TPU v7x, 32 devices: a whole 2x2x4 slice. The times are simulated.
32 devices in a mesh: dp: 2 (over core), seq: 4 (over z), head: 4 (over y, x).
Axes of the slice: x: 2, y: 2, z: 4, core: 2. Of those that a mesh axis runs over, the one named last changes fastest.
Arguments:
- x_in: float32 [2, 512, 1024], P('dp', 'seq'), may hold values from -6 to 6
- cotangent: float32 [2, 512, 1024], P('dp', 'seq'), may hold values from -6 to 6
- attn_gain: bfloat16 [1024], P('seq'), may hold values from 0.25 to 1.75
- w_query: bfloat16 [1024, 512], P('seq', 'head'), may hold values from -0.1875 to 0.1875
- w_key: bfloat16 [1024, 512], P('seq', 'head'), may hold values from -0.1875 to 0.1875
- w_value: bfloat16 [1024, 1024], P('seq', 'head'), may hold values from -0.1875 to 0.1875
- w_outgate: bfloat16 [1024, 1024], P('seq', 'head'), may hold values from -0.1875 to 0.1875
- w_lowrank: bfloat16 [1024, 16], P('seq'), may hold values from -0.1875 to 0.1875
- w_forget: float32 [16, 512], replicated, may hold values from -1.5 to 1.5
- forget_bias: float32 [512], replicated, may hold values from -1 to 6
- group_gain: float32 [256], replicated, may hold values from 0.25 to 1.75
- w_output: bfloat16 [1024, 1024], P('head', 'seq'), may hold values from -0.375 to 0.375
- mlp_gain: bfloat16 [1024], P('seq'), may hold values from 0.25 to 1.75
- w_gate: bfloat16 [1024, 2816], P('seq', 'head'), may hold values from -0.1875 to 0.1875
- w_up: bfloat16 [1024, 2816], P('seq', 'head'), may hold values from -0.1875 to 0.1875
- w_down: bfloat16 [2816, 1024], P('head', 'seq'), may hold values from -0.109375 to 0.109375
Outputs:
- block_out: float32 [2, 512, 1024], P('dp', 'seq')
- grad_input: float32 [2, 512, 1024], P('dp', 'seq')
- grad_attn_gain: float32 [1024], P('seq')
- grad_query: float32 [1024, 512], P('seq', 'head')
- grad_key: float32 [1024, 512], P('seq', 'head')
- grad_value: float32 [1024, 1024], P('seq', 'head')
- grad_outgate: float32 [1024, 1024], P('seq', 'head')
- grad_lowrank: float32 [1024, 16], P('seq')
- grad_forget: float32 [16, 512], replicated
- grad_bias: float32 [512], replicated
- grad_group_gain: float32 [256], replicated
- grad_output: float32 [1024, 1024], P('head', 'seq')
- grad_mlp_gain: float32 [1024], P('seq')
- grad_gate: float32 [1024, 2816], P('seq', 'head')
- grad_up: float32 [1024, 2816], P('seq', 'head')
- grad_down: float32 [2816, 1024], P('head', 'seq')
All inputs are finite; a program needn't handle non-finite values.
Results may differ from a plain program's by a relative error of at most 0.0097.
Values may be sent and summed in bfloat16 or wider, within the bound.
A program may use at most 128 MiB of HBM per device.

v0:
```python
import jax
import jax.numpy as jnp
from jax import lax
from jax.sharding import PartitionSpec as P

DK = 128
DV = 256
SPAN = 64


epsilon = 1e-06
normalizer = 16.0
highest = lax.Precision.HIGHEST


def entering(part, axis, combine, identity, reverse):
    count = lax.axis_size(axis)
    place = lax.axis_index(axis)
    ahead = count - 1 - place if reverse else place
    gathered = jax.tree.map(lambda a: lax.all_gather(a, axis), part)
    state = jax.tree.map(lambda a, e: jnp.zeros_like(a) + jnp.asarray(e, a.dtype), part, identity)

    def one(step, state):
        source = count - 1 - step if reverse else step
        return combine(
            state, jax.tree.map(lambda a: lax.dynamic_index_in_dim(a, source, 0, False), gathered)
        )

    return lax.fori_loop(0, ahead, one, state)


def product(left, right):
    return jnp.dot(left, right, preferred_element_type=jnp.float32)


def rms_rows(inputs):
    return lax.rsqrt(jnp.mean(inputs * inputs, axis=-1, keepdims=True) + epsilon)


def norm_back(inputs, scale, gain, grad):
    scaled = gain * grad
    gain_terms = grad * inputs * scale
    input_grad = scale * scaled - inputs * scale**3 * jnp.mean(
        scaled * inputs, axis=-1, keepdims=True
    )
    return (gain_terms, input_grad)


def compose(earlier, later):
    return (earlier[0] * later[0], later[0][..., None] * earlier[1] + later[1])


def mixer_block(queries, keys_in, values_in, log_decay, start_state):
    block_len = min(SPAN, queries.shape[0])
    blocks = queries.shape[0] // block_len

    def cut(array):
        return array.reshape(blocks, block_len, array.shape[-1])

    lower = jnp.tril(jnp.ones((block_len, block_len), jnp.float32))

    def block_step(carried, pieces):
        query_blk, key_blk, value_blk, decay_blk = pieces
        running = jnp.cumsum(decay_blk, axis=0)
        from_state = jnp.dot(query_blk * jnp.exp(running), carried, precision=highest)
        spread = (
            jnp.exp(jnp.minimum(running[:, None, :] - running[None, :, :], 0.0)) * lower[:, :, None]
        )
        scores = jnp.einsum("id,jd,ijd->ij", query_blk, key_blk, spread, precision=highest)
        inside = jnp.dot(scores, value_blk, precision=highest)
        ending = running[-1]
        weighted = key_blk * jnp.exp(ending[None, :] - running)
        carried = jnp.exp(ending)[:, None] * carried + jnp.dot(
            weighted.T, value_blk, precision=highest
        )
        return (carried, from_state + inside)

    final_state, outputs = lax.scan(
        jax.checkpoint(block_step),
        start_state,
        (cut(queries), cut(keys_in), cut(values_in), cut(log_decay)),
    )
    return (outputs.reshape(queries.shape[0], values_in.shape[-1]), final_state)


def on_device(
    x_in,
    cotangent,
    attn_gain,
    w_query,
    w_key,
    w_value,
    w_outgate,
    w_lowrank,
    w_forget,
    forget_bias,
    group_gain,
    w_output,
    mlp_gain,
    w_gate,
    w_up,
    w_down,
):
    (
        gain_one,
        wq_full,
        wk_full,
        wv_full,
        wg_full,
        wl_full,
        wo_full,
        gain_two,
        wgate_full,
        wup_full,
        wdown_full,
    ) = (
        lax.all_gather(attn_gain, "seq", axis=0, tiled=True),
        lax.all_gather(w_query, "seq", axis=0, tiled=True),
        lax.all_gather(w_key, "seq", axis=0, tiled=True),
        lax.all_gather(w_value, "seq", axis=0, tiled=True),
        lax.all_gather(w_outgate, "seq", axis=0, tiled=True),
        lax.all_gather(w_lowrank, "seq", axis=0, tiled=True),
        lax.all_gather(w_output, "seq", axis=1, tiled=True),
        lax.all_gather(mlp_gain, "seq", axis=0, tiled=True),
        lax.all_gather(w_gate, "seq", axis=0, tiled=True),
        lax.all_gather(w_up, "seq", axis=0, tiled=True),
        lax.all_gather(w_down, "seq", axis=1, tiled=True),
    )
    seqs_here, tok_here, width = x_in.shape
    total_rows = seqs_here * tok_here
    heads_here = wq_full.shape[1] // DK
    key_cols = heads_here * DK
    head_scale = DK ** (-0.5)
    head_pos = lax.axis_index("head")
    forget_cols = lax.dynamic_slice_in_dim(w_forget, head_pos * key_cols, key_cols, 1)
    bias_cols = lax.dynamic_slice_in_dim(forget_bias, head_pos * key_cols, key_cols, 0)
    gain_first = gain_one.astype(jnp.float32)
    gain_second = gain_two.astype(jnp.float32)

    def heads_of(array, size):
        return array.reshape(seqs_here, tok_here, heads_here, size).transpose(0, 2, 1, 3)

    def rows_of(array):
        return array.transpose(0, 2, 1, 3).reshape(total_rows, -1)

    flat_in = x_in.reshape(total_rows, width)
    flat_cot = cotangent.reshape(total_rows, width)
    scale_one = rms_rows(flat_in)
    normed_in = (flat_in * scale_one * gain_first).astype(jnp.bfloat16)
    q_rows = product(normed_in, wq_full)
    k_rows = product(normed_in, wk_full)
    v_rows = product(normed_in, wv_full)
    og_rows = product(normed_in, wg_full)
    low_rank = product(normed_in, wl_full)
    pre_gate = jnp.dot(low_rank, forget_cols, precision=highest) + bias_cols
    log_decay = jax.nn.log_sigmoid(pre_gate) / normalizer
    q_heads = heads_of(q_rows, DK)
    k_heads = heads_of(k_rows, DK)
    v_heads = heads_of(v_rows, DV)
    decay_heads = heads_of(log_decay, DK)
    running = jnp.cumsum(decay_heads, axis=2)
    ending = running[:, :, -1, :]
    decay_total = jnp.exp(ending)
    local_state = jnp.einsum(
        "shld,shlv->shdv",
        k_heads * jnp.exp(ending[:, :, None, :] - running),
        v_heads,
        precision=highest,
    )
    identity = (jnp.ones_like(decay_total), jnp.zeros_like(local_state))
    start_total, start_state = entering((decay_total, local_state), "seq", compose, identity, False)

    def mixed(q_part, k_part, v_part, d_part):
        return jax.vmap(jax.vmap(mixer_block))(
            q_part * head_scale, k_part, v_part, d_part, start_state
        )

    (o_heads, end_state), pullback = jax.vjp(mixed, q_heads, k_heads, v_heads, decay_heads)
    gate_heads = heads_of(og_rows, DV)
    scale_three = rms_rows(o_heads)
    gated_norm = o_heads * scale_three * group_gain
    gate_sig = jax.nn.sigmoid(gate_heads)
    gate_act = gate_heads * gate_sig
    mixed_out = rows_of(gated_norm * gate_act).astype(jnp.bfloat16)
    resid = flat_in + lax.psum(product(mixed_out, wo_full), "head")
    scale_two = rms_rows(resid)
    normed_mid = (resid * scale_two * gain_second).astype(jnp.bfloat16)
    gate_pre = product(normed_mid, wgate_full)
    up_pre = product(normed_mid, wup_full)
    gate_sigma = jax.nn.sigmoid(gate_pre)
    gate_silu = gate_pre * gate_sigma
    mlp_hidden = (gate_silu * up_pre).astype(jnp.bfloat16)
    result = resid + lax.psum(product(mlp_hidden, wdown_full).astype(jnp.bfloat16), "head").astype(
        jnp.float32
    )
    grad_out_b = flat_cot.astype(jnp.bfloat16)
    d_down = product(mlp_hidden.T, grad_out_b)
    d_hidden = product(grad_out_b, wdown_full.T)
    d_gate_pre = (d_hidden * up_pre * gate_sigma * (1.0 + gate_pre * (1.0 - gate_sigma))).astype(
        jnp.bfloat16
    )
    d_up_pre = (d_hidden * gate_silu).astype(jnp.bfloat16)
    d_gate = product(normed_mid.T, d_gate_pre)
    d_up = product(normed_mid.T, d_up_pre)
    d_normed_mid = lax.psum(
        product(d_gate_pre, wgate_full.T) + product(d_up_pre, wup_full.T), "head"
    )
    gain_terms, d_resid_norm = norm_back(resid, scale_two, gain_second, d_normed_mid)
    d_gain_two = jnp.sum(gain_terms, axis=0)
    d_resid = flat_cot + d_resid_norm
    d_resid_b = d_resid.astype(jnp.bfloat16)
    d_output = product(mixed_out.T, d_resid_b)
    d_mixed = heads_of(product(d_resid_b, wo_full.T), DV)
    d_norm_out = d_mixed * gate_act
    d_gate_heads = d_mixed * gated_norm * gate_sig * (1.0 + gate_heads * (1.0 - gate_sig))
    d_group = jnp.sum(d_norm_out * o_heads * scale_three, axis=(0, 1, 2))
    group_terms, d_o_heads = norm_back(o_heads, scale_three, group_gain, d_norm_out)
    state_grad = jnp.einsum(
        "shld,shlv->shdv", q_heads * head_scale * jnp.exp(running), d_o_heads, precision=highest
    )
    later_total, later_grad = entering((decay_total, state_grad), "seq", compose, identity, True)
    d_q, d_k, d_v, d_decay = pullback((d_o_heads, later_grad))
    d_pre = rows_of(d_decay) / normalizer * jax.nn.sigmoid(-pre_gate)
    d_bias = jnp.sum(d_pre, axis=0)
    d_forget = jnp.dot(low_rank.T, d_pre, precision=highest)
    d_low_part = jnp.dot(d_pre, forget_cols.T, precision=highest)
    d_q_b = rows_of(d_q).astype(jnp.bfloat16)
    d_k_b = rows_of(d_k).astype(jnp.bfloat16)
    d_v_b = rows_of(d_v).astype(jnp.bfloat16)
    d_og_b = rows_of(d_gate_heads).astype(jnp.bfloat16)
    d_query = product(normed_in.T, d_q_b)
    d_key = product(normed_in.T, d_k_b)
    d_value = product(normed_in.T, d_v_b)
    d_outgate = product(normed_in.T, d_og_b)
    d_in_part = (
        product(d_q_b, wq_full.T)
        + product(d_k_b, wk_full.T)
        + product(d_v_b, wv_full.T)
        + product(d_og_b, wg_full.T)
    )
    d_in_sum, d_low_sum = lax.psum((d_in_part, d_low_part), "head")
    d_low_b = d_low_sum.astype(jnp.bfloat16)
    d_lowrank = product(normed_in.T, d_low_b)
    d_normed_in = d_in_sum + product(d_low_b, wl_full.T)
    first_terms, d_in_norm = norm_back(flat_in, scale_one, gain_first, d_normed_in)
    d_gain_one = jnp.sum(first_terms, axis=0)
    grad_in = d_resid + d_in_norm
    parts = (
        lax.psum_scatter(d_gain_one, "seq", scatter_dimension=0, tiled=True),
        lax.psum_scatter(d_query, "seq", scatter_dimension=0, tiled=True),
        lax.psum_scatter(d_key, "seq", scatter_dimension=0, tiled=True),
        lax.psum_scatter(d_value, "seq", scatter_dimension=0, tiled=True),
        lax.psum_scatter(d_outgate, "seq", scatter_dimension=0, tiled=True),
        lax.psum_scatter(d_lowrank, "seq", scatter_dimension=0, tiled=True),
        lax.psum_scatter(d_output, "seq", scatter_dimension=1, tiled=True),
        lax.psum_scatter(d_gain_two, "seq", scatter_dimension=0, tiled=True),
        lax.psum_scatter(d_gate, "seq", scatter_dimension=0, tiled=True),
        lax.psum_scatter(d_up, "seq", scatter_dimension=0, tiled=True),
        lax.psum_scatter(d_down, "seq", scatter_dimension=1, tiled=True),
    )
    (
        s_gain_one,
        s_query,
        s_key,
        s_value,
        s_outgate,
        s_lowrank,
        s_output,
        s_gain_two,
        s_gate,
        s_up,
        s_down,
    ) = lax.psum(
        (
            parts[0],
            parts[1],
            parts[2],
            parts[3],
            parts[4],
            parts[5],
            parts[6],
            parts[7],
            parts[8],
            parts[9],
            parts[10],
        ),
        "dp",
    )
    forget_full = lax.dynamic_update_slice_in_dim(
        jnp.zeros(w_forget.shape, jnp.float32), d_forget, head_pos * key_cols, 1
    )
    bias_full = lax.dynamic_update_slice_in_dim(
        jnp.zeros(forget_bias.shape, jnp.float32), d_bias, head_pos * key_cols, 0
    )
    s_forget, s_bias, s_group = lax.psum((forget_full, bias_full, d_group), ("dp", "seq", "head"))
    return (
        result.reshape(seqs_here, tok_here, width),
        grad_in.reshape(seqs_here, tok_here, width),
        s_gain_one,
        s_query,
        s_key,
        s_value,
        s_outgate,
        s_lowrank,
        s_forget,
        s_bias,
        s_group,
        s_output,
        s_gain_two,
        s_gate,
        s_up,
        s_down,
    )


def solution(mesh):
    return jax.shard_map(
        on_device,
        mesh=mesh,
        in_specs=(
            P("dp", "seq", None),
            P("dp", "seq", None),
            P("seq"),
            P("seq", "head"),
            P("seq", "head"),
            P("seq", "head"),
            P("seq", "head"),
            P("seq", None),
            P(),
            P(),
            P(),
            P("head", "seq"),
            P("seq"),
            P("seq", "head"),
            P("seq", "head"),
            P("head", "seq"),
        ),
        out_specs=(
            P("dp", "seq", None),
            P("dp", "seq", None),
            P("seq"),
            P("seq", "head"),
            P("seq", "head"),
            P("seq", "head"),
            P("seq", "head"),
            P("seq", None),
            P(),
            P(),
            P(),
            P("head", "seq"),
            P("seq"),
            P("seq", "head"),
            P("seq", "head"),
            P("head", "seq"),
        ),
        check_vma=False,
    )
```

profile of v0, /device:TPU:0, one launch (start us, length us, event | category | flops | bytes accessed | tf_op | source)
XLA Modules:
  0.0 774.9 jit_solution(1150083508637122755)
XLA Ops:
  10.6 12.6 %all-gather.2 = bf16[4,1,256]{2,1,0:T(2,128)(2,1)S(1)} all-gather(bf16[1,1,256]{2,1,0:T(2,128)(2,1)S(1)} %reshape.777), channel_id=1, replica_groups=mesh['dp'=2,'seq'=4,'head'=4] {'seq'}, dimensions={0}, use_global_device_ids=true | all-gather | bytes 2560 | tf_op jit(solution)/shard_map/all_gather | solution.py:117
  23.2 13.3 %all_gather.52 = bf16[1024,16]{0,1:T(8,128)(2,1)S(1)} all-gather(bf16[256,16]{0,1:T(8,128)(2,1)} %param.31), channel_id=1, replica_groups=mesh['dp'=2,'seq'=4,'head'=4] {'seq'}, dimensions={0}, use_global_device_ids=true | all-gather | bytes 40960 | tf_op jit(solution)/shard_map/all_gather | solution.py:122
  39.2 15.9 %all_gather.55 = bf16[1024,256]{1,0:T(8,128)(2,1)S(1)} all-gather(bf16[256,256]{1,0:T(8,128)(2,1)S(1)} %copy-done.37), channel_id=1, replica_groups=mesh['dp'=2,'seq'=4,'head'=4] {'seq'}, dimensions={0}, use_global_device_ids=true | all-gather | bytes 655360 | tf_op jit(solution)/shard_map/all_gather | solution.py:120
  55.4 14.5 %all_gather.54 = bf16[1024,128]{1,0:T(8,128)(2,1)S(1)} all-gather(bf16[256,128]{1,0:T(8,128)(2,1)S(1)} %copy-done.41), channel_id=1, replica_groups=mesh['dp'=2,'seq'=4,'head'=4] {'seq'}, dimensions={0}, use_global_device_ids=true | all-gather | bytes 327680 | tf_op jit(solution)/shard_map/all_gather | solution.py:119
  70.5 15.0 %all-gather = f32[512,256]{1,0:T(8,128)S(1)} all-gather(f32[128,256]{1,0:T(8,128)S(1)} %fusion.104), channel_id=2, replica_groups=mesh['dp'=2,'seq'=4,'head'=4] {'seq'}, dimensions={0}, use_global_device_ids=true | all-gather | bytes 655360 | tf_op jit(solution)/shard_map/all_gather | solution.py:20
  85.5 8.7 %all_gather.53 = f32[4,1,1,128]{3,2,1,0:T(1,128)S(1)} all-gather(f32[1,1,1,128]{3,2,1,0:T(1,128)S(1)} %get-tuple-element.745), channel_id=1, replica_groups=mesh['dp'=2,'seq'=4,'head'=4] {'seq'}, dimensions={0}, use_global_device_ids=true | all-gather | bytes 2560 | tf_op jit(solution)/shard_map/all_gather | solution.py:20
  94.2 14.6 %all_gather.58 = bf16[1024,128]{1,0:T(8,128)(2,1)S(1)} all-gather(bf16[256,128]{1,0:T(8,128)(2,1)S(1)} %copy-done.42), channel_id=1, replica_groups=mesh['dp'=2,'seq'=4,'head'=4] {'seq'}, dimensions={0}, use_global_device_ids=true | all-gather | bytes 327680 | tf_op jit(solution)/shard_map/all_gather | solution.py:118
  109.6 6.8 while.70
  117.1 15.5 %all_gather.59 = bf16[1024,256]{1,0:T(8,128)(2,1)S(1)} all-gather(bf16[256,256]{1,0:T(8,128)(2,1)S(1)} %copy-done.38), channel_id=1, replica_groups=mesh['dp'=2,'seq'=4,'head'=4] {'seq'}, dimensions={0}, use_global_device_ids=true | all-gather | bytes 655360 | tf_op jit(solution)/shard_map/all_gather | solution.py:121
  132.6 14.8 %all_gather.60 = bf16[256,1024]{1,0:T(8,128)(2,1)S(1)} all-gather(bf16[256,256]{1,0:T(8,128)(2,1)S(1)} %copy-done.39), channel_id=1, replica_groups=mesh['dp'=2,'seq'=4,'head'=4] {'seq'}, dimensions={1}, use_global_device_ids=true | all-gather | bytes 655360 | tf_op jit(solution)/shard_map/all_gather | solution.py:123
  151.2 8.8 %all-gather.3 = bf16[4,1,256]{2,1,0:T(2,128)(2,1)S(1)} all-gather(bf16[1,1,256]{2,1,0:T(2,128)(2,1)S(1)} %reshape.779), channel_id=1, replica_groups=mesh['dp'=2,'seq'=4,'head'=4] {'seq'}, dimensions={0}, use_global_device_ids=true | all-gather | bytes 2560 | tf_op jit(solution)/shard_map/all_gather | solution.py:124
  161.1 32.6 %all-reduce.13.cloned.1.call-done = f32[128,1024]{1,0:T(8,128)} async-done(((f32[128,1024]{1,0:T(8,128)}), f32[128,1024]{1,0:T(8,128)}) %all-reduce.13.cloned.1.call-update) | async-done | bytes 524304 | tf_op jit(solution)/shard_map/psum | solution.py:185
  195.6 2.7 fusion.132
  198.3 22.5 %all-gather.10.cloned.1.call-done = bf16[1024,704]{0,1:T(8,128)(2,1)} async-done(((bf16[256,704]{0,1:T(8,128)(2,1)}), bf16[1024,704]{0,1:T(8,128)(2,1)}) %all-gather.10.cloned.1.call-update) | async-done | bytes 1441808 | tf_op jit(solution)/shard_map/all_gather | solution.py:126
  220.8 2.6 fusion.133
  223.4 32.5 %all-gather.12.cloned.1.call-done = bf16[704,1024]{1,0:T(8,128)(2,1)} async-done(((bf16[704,256]{1,0:T(8,128)(2,1)}), bf16[704,1024]{1,0:T(8,128)(2,1)}) %all-gather.12.cloned.1.call-update) | async-done | bytes 1441808 | tf_op jit(solution)/shard_map/all_gather | solution.py:127
  263.4 40.4 %all-reduce.17.cloned.1.call-done = f32[128,1024]{1,0:T(8,128)} async-done(((f32[128,1024]{1,0:T(8,128)}), f32[128,1024]{1,0:T(8,128)}) %all-reduce.17.cloned.1.call-update) | async-done | bytes 524304 | tf_op jit(solution)/shard_map/psum | solution.py:205
  305.6 44.8 %all-reduce.15.cloned.1.call-done = bf16[128,1024]{1,0:T(8,128)(2,1)} async-done(((bf16[128,1024]{1,0:T(8,128)(2,1)}), bf16[128,1024]{1,0:T(8,128)(2,1)}) %all-reduce.15.cloned.1.call-update) | async-done | bytes 262160 | tf_op jit(solution)/shard_map/psum | solution.py:193
  352.7 2.6 fusion.94
  355.7 15.3 %all-gather.1 = f32[512,256]{1,0:T(8,128)S(1)} all-gather(f32[128,256]{1,0:T(8,128)S(1)} %fusion.107), channel_id=3, replica_groups=mesh['dp'=2,'seq'=4,'head'=4] {'seq'}, dimensions={0}, use_global_device_ids=true | all-gather | bytes 655360 | tf_op jit(solution)/shard_map/all_gather | solution.py:20
  374.3 19.5 %while.71 = (s32[]{:T(128)}, f32[1,1,128,256]{2,3,1,0:T(8,128)S(1)}, f32[2,1,1,64,128]{4,3,2,1,0:T(8,128)S(1)}, bf16[2,1,1,64,128]{4,3,2,1,0:T(8,128)(2,1)}, bf1...) while((s32[]{:T(128)}, ...), condition=%wide.region_23.24_spmd.clone.clone, body=%wide.region_16.23_spmd.clone.sunk.clone | while | flops 141848576 | bytes 4776213 | solution.py:78
  413.6 9.2 %psum.137 = bf16[128,16]{0,1:T(8,128)(2,1)S(1)} all-reduce(f32[128,16]{0,1:T(8,128)S(1)} %fusion.111), channel_id=1, replica_groups=mesh['dp'=2,'seq'=4,'head'=4] {'head'}, use_global_device_ids=true, to_apply=%region_25.26 | all-reduce | flops 2048 | bytes 12288 | tf_op jit(solution)/shard_map/psum | solution.py:241
  423.7 15.4 %reduce-scatter.12.cloned.1.call-done = f32[256,128]{1,0:T(8,128)} async-done(((f32[1024,128]{1,0:T(8,128)}), f32[256,128]{1,0:T(8,128)}) %reduce-scatter.12.cloned.1.call-update) | async-done | bytes 131088 | tf_op jit(solution)/shard_map/reduce_scatter | solution.py:251
  439.2 27.9 %reduce-scatter.20.cloned.1.call-done = f32[256,256]{1,0:T(8,128)} async-done(((f32[256,1024]{1,0:T(8,128)}), f32[256,256]{1,0:T(8,128)}) %reduce-scatter.20.cloned.1.call-update) | async-done | bytes 262160 | tf_op jit(solution)/shard_map/reduce_scatter | solution.py:255
  467.1 27.9 %reduce-scatter.14.cloned.1.call-done = f32[256,256]{1,0:T(8,128)} async-done(((f32[1024,256]{1,0:T(8,128)}), f32[256,256]{1,0:T(8,128)}) %reduce-scatter.14.cloned.1.call-update) | async-done | bytes 262160 | tf_op jit(solution)/shard_map/reduce_scatter | solution.py:252
  495.0 27.9 %reduce-scatter.16.cloned.1.call-done = f32[256,256]{1,0:T(8,128)} async-done(((f32[1024,256]{1,0:T(8,128)}), f32[256,256]{1,0:T(8,128)}) %reduce-scatter.16.cloned.1.call-update) | async-done | bytes 262160 | tf_op jit(solution)/shard_map/reduce_scatter | solution.py:253
  522.9 57.0 %reduce-scatter.22.cloned.1.call-done = f32[256,704]{0,1:T(8,128)} async-done(((f32[1024,704]{0,1:T(8,128)}), f32[256,704]{0,1:T(8,128)}) %reduce-scatter.22.cloned.1.call-update) | async-done | bytes 720912 | tf_op jit(solution)/shard_map/reduce_scatter | solution.py:257
  579.9 58.4 %reduce-scatter.24.cloned.1.call-done = f32[256,704]{0,1:T(8,128)} async-done(((f32[1024,704]{0,1:T(8,128)}), f32[256,704]{0,1:T(8,128)}) %reduce-scatter.24.cloned.1.call-update) | async-done | bytes 720912 | tf_op jit(solution)/shard_map/reduce_scatter | solution.py:258
  638.2 58.2 %reduce-scatter.26.cloned.1.call-done = f32[704,256]{1,0:T(8,128)} async-done(((f32[704,1024]{1,0:T(8,128)}), f32[704,256]{1,0:T(8,128)}) %reduce-scatter.26.cloned.1.call-update) | async-done | bytes 720912 | tf_op jit(solution)/shard_map/reduce_scatter | solution.py:259
  698.2 40.7 %all-reduce.3 = (f32[16,512]{1,0:T(8,128)}, f32[512]{0:T(512)}, f32[256]{0:T(256)}) all-reduce(f32[16,512]{1,0:T(8,128)S(1)} %convolution_dynamic-update-slice_fusion, f32[512]{0:T(512)S(1)} %dynamic_update_slice.52, f32[256]{0:T(256)S(1)} %copy-done.48), channel_id=1, replica_groups=mesh['dp'=2,'seq'=4,'head'=4] {'dp','seq','head'}, use_global_device_ids=true, to_apply=%region_40.41 | all-reduce | flops 8960 | bytes 71680 | tf_op jit(solution)/shard_map/psum | solution.py:295
  740.3 10.8 %all-reduce.4 = (f32[1024]{0:T(1024)S(1)}, f32[1024]{0:T(1024)S(1)}) all-reduce(f32[1024]{0:T(1024)S(1)} %get-tuple-element.643, f32[1024]{0:T(1024)S(1)} %copy-done.43), channel_id=4, replica_groups=mesh['dp'=2,'seq'=4,'head'=4] {'seq'}, use_global_device_ids=true, to_apply=%region_28.29.clone | all-reduce | flops 2048 | bytes 16384
  751.3 4.6 all-reduce.5
  (317 shorter events, 92.1 us)
Async XLA Ops:
  8.0 47.3 %copy-start.41 = (bf16[256,128]{1,0:T(8,128)(2,1)S(1)}, bf16[256,128]{1,0:T(8,128)(2,1)}, u32[]{:S(2)}) copy-start(bf16[256,128]{1,0:T(8,128)(2,1)} %param.28) | copy-start | bytes 196612
  8.0 185.7 %all-reduce.13.cloned.1.call-start = ((), (), s32[]{:S(2)}) async-start(), calls=%async_computation.9 | async-start | bytes 1048576 | tf_op jit(solution)/shard_map/psum | solution.py:185
  9.9 250.8 %copy-start.44 = (f32[128]{0:T(128)}, f32[128]{0:T(128)S(1)}, u32[]{:S(2)}) copy-start(f32[128]{0:T(128)S(1)} %get-tuple-element.747) | copy-start | bytes 1540
  39.0 55.2 %copy-start.24 = (f32[128,128]{1,0:T(8,128)}, f32[128,128]{1,0:T(8,128)S(1)}, u32[]{:S(2)}) copy-start(f32[128,128]{1,0:T(8,128)S(1)} %convolution_add_fusion.7) | copy-start | bytes 196612
  55.4 38.8 %copy-start.42 = (bf16[256,128]{1,0:T(8,128)(2,1)S(1)}, bf16[256,128]{1,0:T(8,128)(2,1)}, u32[]{:S(2)}) copy-start(bf16[256,128]{1,0:T(8,128)(2,1)} %param.27) | copy-start | bytes 196612
  117.1 43.5 %copy-start.50 = (f32[128]{0:T(128)}, f32[128]{0:T(128)S(1)}, u32[]{:S(2)}) copy-start(f32[128]{0:T(128)S(1)} %rsqrt.38) | copy-start | bytes 1540
  147.4 47.5 %copy-start.11 = (bf16[256,1024]{1,0:T(8,128)(2,1)}, bf16[256,1024]{1,0:T(8,128)(2,1)S(1)}, u32[]{:S(2)}) copy-start(bf16[256,1024]{1,0:T(8,128)(2,1)S(1)} %all_gather.60) | copy-start | bytes 1572868
  147.4 46.3 %copy-start.1 = (f32[1,128,1024]{2,1,0:T(8,128)S(1)}, f32[1,128,1024]{2,1,0:T(8,128)}, u32[]{:S(2)}) copy-start(f32[1,128,1024]{2,1,0:T(8,128)} %param.24) | copy-start | bytes 1572868
  149.4 46.2 %all-gather.8.cloned.1.call-start = ((), (), s32[]{:S(2)}) async-start(), calls=%async_computation.10 | async-start | bytes 1802240 | tf_op jit(solution)/shard_map/all_gather | solution.py:125
  149.9 70.9 %all-gather.10.cloned.1.call-start = ((), (), s32[]{:S(2)}) async-start(), calls=%async_computation.11 | async-start | bytes 1802240 | tf_op jit(solution)/shard_map/all_gather | solution.py:126
  150.5 105.4 %all-gather.12.cloned.1.call-start = ((), (), s32[]{:S(2)}) async-start(), calls=%async_computation.12 | async-start | bytes 1802240 | tf_op jit(solution)/shard_map/all_gather | solution.py:127
  151.1 152.7 %all-reduce.17.cloned.1.call-start = ((), (), s32[]{:S(2)}) async-start(), calls=%async_computation.14 | async-start | bytes 1048576 | tf_op jit(solution)/shard_map/psum | solution.py:205
  195.5 60.4 %copy-start.12 = (f32[1,128,1024]{2,1,0:T(8,128)S(1)}, f32[1,128,1024]{2,1,0:T(8,128)}, u32[]{:S(2)}) copy-start(f32[1,128,1024]{2,1,0:T(8,128)} %param.25) | copy-start | bytes 1572868
  260.1 90.3 %all-reduce.15.cloned.1.call-start = ((), (), s32[]{:S(2)}) async-start(), calls=%async_computation.13 | async-start | bytes 524288 | tf_op jit(solution)/shard_map/psum | solution.py:193
  263.3 89.4 %copy-start.30 = (f32[2,1,1,64,256]{4,3,2,1,0:T(8,128)S(1)}, f32[2,1,1,64,256]{4,3,2,1,0:T(8,128)}, u32[]{:S(2)}) copy-start(f32[2,1,1,64,256]{4,3,2,1,0:T(8,128)} %copy-done.29) | copy-start | bytes 393220
  263.3 89.4 %copy-start.51 = (f32[128]{0:T(128)S(1)}, f32[128]{0:T(128)}, u32[]{:S(2)}) copy-start(f32[128]{0:T(128)} %copy-done.50) | copy-start | bytes 1540
  263.4 160.4 %reduce-scatter.10.cloned.1.call-start = ((), (), s32[]{:S(2)}) async-start(), calls=%async_computation.16 | async-start | bytes 655360 | tf_op jit(solution)/shard_map/reduce_scatter | solution.py:250
  395.8 43.4 %reduce-scatter.12.cloned.1.call-start = ((), (), s32[]{:S(2)}) async-start(), calls=%async_computation.17 | async-start | bytes 655360 | tf_op jit(solution)/shard_map/reduce_scatter | solution.py:251
  397.7 69.4 %reduce-scatter.20.cloned.1.call-start = ((), (), s32[]{:S(2)}) async-start(), calls=%async_computation.21 | async-start | bytes 1310720 | tf_op jit(solution)/shard_map/reduce_scatter | solution.py:255
  399.1 95.8 %reduce-scatter.14.cloned.1.call-start = ((), (), s32[]{:S(2)}) async-start(), calls=%async_computation.18 | async-start | bytes 1310720 | tf_op jit(solution)/shard_map/reduce_scatter | solution.py:252
  400.5 122.3 %reduce-scatter.16.cloned.1.call-start = ((), (), s32[]{:S(2)}) async-start(), calls=%async_computation.19 | async-start | bytes 1310720 | tf_op jit(solution)/shard_map/reduce_scatter | solution.py:253
  401.9 178.0 %reduce-scatter.22.cloned.1.call-start = ((), (), s32[]{:S(2)}) async-start(), calls=%async_computation.22 | async-start | bytes 3604480 | tf_op jit(solution)/shard_map/reduce_scatter | solution.py:257
  404.1 234.1 %reduce-scatter.24.cloned.1.call-start = ((), (), s32[]{:S(2)}) async-start(), calls=%async_computation.23 | async-start | bytes 3604480 | tf_op jit(solution)/shard_map/reduce_scatter | solution.py:258
  407.2 289.3 %reduce-scatter.26.cloned.1.call-start = ((), (), s32[]{:S(2)}) async-start(), calls=%async_computation.24 | async-start | bytes 3604480 | tf_op jit(solution)/shard_map/reduce_scatter | solution.py:259
  410.4 328.5 %all-reduce.19.cloned.1.call-start = ((), (), s32[]{:S(2)}) async-start(), calls=%async_computation.15 | async-start | bytes 1048576 | tf_op jit(solution)/shard_map/psum | solution.py:241
  413.3 283.2 %copy-start.54 = (u32[32]{0:T(128)S(1)}, u32[32]{0:T(128)}, u32[]{:S(2)}) copy-start(u32[32]{0:T(128)} %constant.207) | copy-start | bytes 388
  413.3 284.9 %copy-start.48 = (f32[256]{0:T(256)S(1)}, f32[256]{0:T(256)}, u32[]{:S(2)}) copy-start(f32[256]{0:T(256)} %get-tuple-element.645) | copy-start | bytes 3076
  413.3 325.6 %copy-start.45 = (f32[128]{0:T(128)S(1)}, f32[128]{0:T(128)}, u32[]{:S(2)}) copy-start(f32[128]{0:T(128)} %copy-done.44) | copy-start | bytes 1540
  413.3 338.0 %reduce-scatter.18.cloned.1.call-start = ((), (), s32[]{:S(2)}) async-start(), calls=%async_computation.20 | async-start | bytes 81920 | tf_op jit(solution)/shard_map/reduce_scatter | solution.py:254
  423.6 333.2 %all-reduce.21.cloned.1.call-start = ((), (), s32[]{:S(2)}) async-start(), calls=%async_computation.25 | async-start | bytes 6422528 | tf_op jit(solution)/shard_map/psum | solution.py:273
  696.5 43.9 %copy-start.43 = (f32[1024]{0:T(1024)S(1)}, f32[1024]{0:T(1024)}, u32[]{:S(2)}) copy-start(f32[1024]{0:T(1024)} %get-tuple-element.641) | copy-start | bytes 12292
  696.5 59.4 %copy-start.49 = (f32[128]{0:T(128)S(1)}, f32[128]{0:T(128)}, u32[]{:S(2)}) copy-start(f32[128]{0:T(128)} %get-tuple-element.746) | copy-start | bytes 1540
  (44 other events, 354.5 us)
Sparse Core Ops, SparseCore 0:
  149.5 44.1 all-reduce.12
  260.2 43.5 all-reduce.16
  307.3 43.0 all-reduce.14
  414.5 43.8 all-reduce.18
  696.6 23.7 all-reduce.20
Sparse Core Ops, SparseCore 1:
  151.4 34.3 all-gather.7
  187.1 33.6 all-gather.9
  222.2 33.6 all-gather.11
  395.8 20.2 reduce-scatter.9
  419.0 20.1 reduce-scatter.11
  441.5 25.5 reduce-scatter.19
  469.2 25.7 reduce-scatter.13
  497.1 25.7 reduce-scatter.15
  525.1 54.8 reduce-scatter.21
  582.2 56.0 reduce-scatter.23
  640.4 56.0 reduce-scatter.25
  699.3 18.9 reduce-scatter.17
where the time goes:
time: 776 us; the launch traced here: 775 us
  waiting for transfers between devices  447 us (58%)
  blocking collectives  214 us (28%)
  matrix products  40.4 us (5%)
  other arithmetic  28.8 us (4%)
  local copies, waits for them, and re-layouts  25.7 us (3%)
  between operations  16.7 us (2%)
    reduce_scatter x1, waiting for transfers between devices, on_device(): lax.psum_scatter(d_up, 'seq', scatter_dimension=0, tiled=True)  58.4 us
    reduce_scatter x1, waiting for transfers between devices, on_device(): lax.psum_scatter(d_down, 'seq', scatter_dimension=1, tiled=True)  58.2 us
    reduce_scatter x1, waiting for transfers between devices, on_device(): lax.psum_scatter(d_gate, 'seq', scatter_dimension=0, tiled=True)  57 us
    psum x1, waiting for transfers between devices, on_device(): lax.psum(product(mlp_hidden, wdown_full).astype(jnp.bfloat16), 'head')  44.8 us
    psum x1, blocking collectives, on_device(): lax.psum((forget_full, bias_full, d_group), ('dp', 'seq', 'head'))  40.7 us
    psum x1, waiting for transfers between devices, on_device(): lax.psum(product(d_gate_pre, wgate_full.T) + product(d_up_pre, wup_full.T...  40.4 us
    all_gather x3, blocking collectives, entering(): gathered = jax.tree.map(lambda a: lax.all_gather(a, axis), part)  39 us
    dot_general x27, matrix products, product(): return jnp.dot(left, right, preferred_element_type=jnp.float32)  34.3 us
  transfers between devices with their start and end apart: 17, of which 12 were waited for; matrix products, arithmetic and copies ran while one was open for 4% of the time, Pallas kernels for 0%

commit v1 on v0

v1 whole, which is shorter than its diff:
```python
import jax
import jax.numpy as jnp
from jax import lax
from jax.experimental import pallas as pl
from jax.experimental.pallas import tpu as pltpu
from jax.sharding import PartitionSpec as P

DK = 128
DV = 256
SPAN = 64


epsilon = 1e-06
normalizer = 16.0
highest = lax.Precision.HIGHEST


def exchange(items, cid):
    axes = []
    for kind, axis, _ in items:
        for name in axis if kind == "wg" else (axis,):
            if name not in axes:
                axes.append(name)
    size = {name: lax.axis_size(name) for name in axes}
    out_shape, scratch = [], []
    for kind, axis, arr in items:
        if kind == "ag":
            out_shape.append(jax.ShapeDtypeStruct((size[axis],) + arr.shape, arr.dtype))
        elif kind == "wg":
            out_shape.append(jax.ShapeDtypeStruct((size[axis[0]],) + arr.shape, arr.dtype))
        else:
            out_shape.append(jax.ShapeDtypeStruct(arr.shape, arr.dtype))
        n = size[axis[0]] if kind == "wg" else size[axis]
        scratch.append(pltpu.SemaphoreType.DMA((2, n)))
        if kind == "ar":
            scratch.append(pltpu.SemaphoreType.DMA((2, n)))
            scratch.append(pltpu.VMEM(arr.shape, arr.dtype))
        elif kind == "wg":
            scratch.append(pltpu.SemaphoreType.DMA((2, n, size[axis[1]])))
        if kind != "ar":
            scratch.append(pltpu.SemaphoreType.DMA)

    def kernel(*refs):
        count = len(items)
        ins, outs, rest = refs[:count], refs[count : 2 * count], list(refs[2 * count :])
        me = {name: lax.axis_index(name) for name in axes}
        barrier = pltpu.get_barrier_semaphore()
        for name in axes:
            for k in range(1, size[name]):
                peer = lax.rem(me[name] + k, size[name])
                pl.semaphore_signal(
                    barrier, inc=1, device_id={name: peer}, device_id_type=pl.DeviceIdType.MESH
                )
        pl.semaphore_wait(barrier, sum(size[name] - 1 for name in axes))

        def remote(source, target, sems, k, name, peer):
            return pltpu.make_async_remote_copy(
                src_ref=source,
                dst_ref=target,
                send_sem=sems.at[(0,) + k],
                recv_sem=sems.at[(1,) + k],
                device_id={name: peer},
                device_id_type=pl.DeviceIdType.MESH,
            )

        waits, later = [], []
        for (kind, axis, arr), src, dst in zip(items, ins, outs):
            sems = rest.pop(0)
            name = axis[0] if kind == "wg" else axis
            n, here = size[name], me[name]
            if kind == "ar":
                sems_two, land = rest.pop(0), rest.pop(0)
                sent = []
                for k in range(1, n):
                    peer = lax.rem(here + k, n)
                    came = lax.rem(here + n - k, n)
                    copy = remote(src.at[peer], land.at[here], sems, (k,), name, peer)
                    copy.start()
                    sent.append((copy, remote(land.at[came], land.at[came], sems, (k,), name, peer)))
                later.append(("ar", src, dst, land, sems_two, name, n, here, sent))
                continue
            if kind == "wg":
                sems_two = rest.pop(0)
            local = rest.pop(0)
            if kind == "wg":
                other = axis[1]
                part = arr.shape[0] // size[other]
                rows = pl.ds(pl.multiple_of(me[other] * part, part), part)
                own = pltpu.make_async_copy(src, dst.at[here], local)
                own.start()
                waits.append(own.wait)
                sent = []
                for k in range(1, n):
                    peer = lax.rem(here + k, n)
                    came = lax.rem(here + n - k, n)
                    copy = remote(src.at[rows], dst.at[here, rows], sems, (k,), name, peer)
                    copy.start()
                    arrived = dst.at[came, rows]
                    sent.append((copy, remote(arrived, arrived, sems, (k,), name, peer), came))
                later.append(("wg", dst, sems_two, other, part, rows, sent))
                continue
            piece = src if kind == "ag" else src.at[here]
            own = pltpu.make_async_copy(piece, dst.at[here], local)
            own.start()
            waits.append(own.wait)
            for k in range(1, n):
                peer = lax.rem(here + k, n)
                came = lax.rem(here + n - k, n)
                piece = src if kind == "ag" else src.at[peer]
                copy = remote(piece, dst.at[here], sems, (k,), name, peer)
                copy.start()
                waits.append(copy.wait_send)
                waits.append(remote(dst.at[came], dst.at[came], sems, (k,), name, peer).wait_recv)
        for entry in later:
            if entry[0] == "ar":
                _, src, dst, land, sems_two, name, n, here, sent = entry
                total = src[here].astype(jnp.float32)
                for k, (copy, arrival) in enumerate(sent, 1):
                    arrival.wait_recv()
                    came = lax.rem(here + n - k, n)
                    total = total + land[came].astype(jnp.float32)
                dst[here] = total.astype(dst.dtype)
                for k in range(1, n):
                    peer = lax.rem(here + k, n)
                    came = lax.rem(here + n - k, n)
                    copy = remote(dst.at[here], dst.at[here], sems_two, (k,), name, peer)
                    copy.start()
                    waits.append(copy.wait_send)
                    waits.append(
                        remote(dst.at[came], dst.at[came], sems_two, (k,), name, peer).wait_recv
                    )
                for copy, _ in sent:
                    waits.append(copy.wait_send)
            else:
                _, dst, sems_two, other, part, rows, sent = entry
                m, place = size[other], me[other]
                for k, (copy, arrival, came) in enumerate(sent, 1):
                    arrival.wait_recv()
                    waits.append(copy.wait_send)
                    for j in range(1, m):
                        partner = lax.rem(place + j, m)
                        whose = lax.rem(place + m - j, m)
                        theirs = dst.at[came, pl.ds(pl.multiple_of(whose * part, part), part)]
                        piece = dst.at[came, rows]
                        onward = remote(piece, piece, sems_two, (k, j), other, partner)
                        onward.start()
                        waits.append(onward.wait_send)
                        waits.append(
                            remote(theirs, theirs, sems_two, (k, j), other, partner).wait_recv
                        )
        for wait in waits:
            wait()

    vmem = pl.BlockSpec(memory_space=pltpu.VMEM)
    return pl.pallas_call(
        kernel,
        out_shape=out_shape,
        in_specs=[vmem] * len(items),
        out_specs=[vmem] * len(items),
        scratch_shapes=scratch,
        compiler_params=pltpu.CompilerParams(
            collective_id=cid, has_side_effects=True, vmem_limit_bytes=60 * 1024 * 1024
        ),
    )(*[item[2] for item in items])


def dot_t(left, right):
    return lax.dot_general(
        left, right, (((1,), (1,)), ((), ())), preferred_element_type=jnp.float32
    )


def dot_rows(left, right):
    return lax.dot_general(
        left, right, (((0,), (0,)), ((), ())), preferred_element_type=jnp.float32
    )


def product(left, right):
    return jnp.dot(left, right, preferred_element_type=jnp.float32)


def rms_rows(inputs):
    return lax.rsqrt(jnp.mean(inputs * inputs, axis=-1, keepdims=True) + epsilon)


def norm_back(inputs, scale, gain, grad):
    scaled = gain * grad
    gain_terms = grad * inputs * scale
    input_grad = scale * scaled - inputs * scale**3 * jnp.mean(
        scaled * inputs, axis=-1, keepdims=True
    )
    return (gain_terms, input_grad)


def mixer_block(queries, keys_in, values_in, log_decay, start_state):
    block_len = min(SPAN, queries.shape[0])
    blocks = queries.shape[0] // block_len

    def cut(array):
        return array.reshape(blocks, block_len, array.shape[-1])

    lower = jnp.tril(jnp.ones((block_len, block_len), jnp.float32))

    def block_step(carried, pieces):
        query_blk, key_blk, value_blk, decay_blk = pieces
        running = jnp.cumsum(decay_blk, axis=0)
        from_state = jnp.dot(query_blk * jnp.exp(running), carried, precision=highest)
        spread = (
            jnp.exp(jnp.minimum(running[:, None, :] - running[None, :, :], 0.0)) * lower[:, :, None]
        )
        scores = jnp.einsum("id,jd,ijd->ij", query_blk, key_blk, spread, precision=highest)
        inside = jnp.dot(scores, value_blk, precision=highest)
        ending = running[-1]
        weighted = key_blk * jnp.exp(ending[None, :] - running)
        carried = jnp.exp(ending)[:, None] * carried + jnp.dot(
            weighted.T, value_blk, precision=highest
        )
        return (carried, from_state + inside)

    final_state, outputs = lax.scan(
        jax.checkpoint(block_step),
        start_state,
        (cut(queries), cut(keys_in), cut(values_in), cut(log_decay)),
    )
    return (outputs.reshape(queries.shape[0], values_in.shape[-1]), final_state)


def on_device(
    x_in,
    cotangent,
    attn_gain,
    w_query,
    w_key,
    w_value,
    w_outgate,
    w_lowrank,
    w_forget,
    forget_bias,
    group_gain,
    w_output,
    mlp_gain,
    w_gate,
    w_up,
    w_down,
):
    seqs_here, tok_here, width = x_in.shape
    total_rows = seqs_here * tok_here
    bf16, f32 = jnp.bfloat16, jnp.float32
    n_seq, n_head, n_dp = lax.axis_size("seq"), lax.axis_size("head"), lax.axis_size("dp")
    seq_pos, head_pos, dp_pos = (
        lax.axis_index("seq"),
        lax.axis_index("head"),
        lax.axis_index("dp"),
    )
    shard_rows = w_query.shape[0]
    part_rows = shard_rows // n_dp
    key_cols, val_cols, hidden = w_query.shape[1], w_value.shape[1], w_gate.shape[1]
    rank = w_lowrank.shape[1]
    heads_here = key_cols // DK
    head_scale = DK ** (-0.5)
    side = -(-(rank + 2) // 128) * 128
    packed = jnp.concatenate(
        (
            w_query,
            w_key,
            w_value,
            w_outgate,
            w_lowrank,
            attn_gain[:, None],
            mlp_gain[:, None],
            jnp.zeros((shard_rows, side - rank - 2), bf16),
            w_output.T,
            w_gate,
            w_up,
            w_down.T,
        ),
        axis=1,
    )
    (weights,) = exchange([("wg", ("seq", "dp"), packed)], 0)
    weights = weights.reshape(width, -1)
    attn_cols = 2 * key_cols + 2 * val_cols
    w_attn = weights[:, :attn_cols]
    w_low = weights[:, attn_cols : attn_cols + side]
    wl_full = w_low[:, :rank]
    gain_first = w_low[:, rank].astype(f32)
    gain_second = w_low[:, rank + 1].astype(f32)
    at = attn_cols + side
    wo_t = weights[:, at : at + val_cols]
    at = at + val_cols
    w_gu = weights[:, at : at + 2 * hidden]
    wdown_t = weights[:, at + 2 * hidden :]
    forget_cols = lax.dynamic_slice_in_dim(w_forget, head_pos * key_cols, key_cols, 1)
    bias_cols = lax.dynamic_slice_in_dim(forget_bias, head_pos * key_cols, key_cols, 0)

    def heads_of(array, size):
        return array.reshape(seqs_here, tok_here, heads_here, size).transpose(0, 2, 1, 3)

    def rows_of(array):
        return array.transpose(0, 2, 1, 3).reshape(total_rows, -1)

    def spread_head(array):
        return array.astype(bf16).reshape(n_head, array.shape[0] // n_head, array.shape[1])

    flat_in = x_in.reshape(total_rows, width)
    flat_cot = cotangent.reshape(total_rows, width)
    scale_one = rms_rows(flat_in)
    normed_in = (flat_in * scale_one * gain_first).astype(bf16)
    proj = product(normed_in, w_attn)
    q_rows = proj[:, :key_cols]
    k_rows = proj[:, key_cols : 2 * key_cols]
    v_rows = proj[:, 2 * key_cols : 2 * key_cols + val_cols]
    og_rows = proj[:, 2 * key_cols + val_cols :]
    low_rank = product(normed_in, wl_full)
    pre_gate = jnp.dot(low_rank, forget_cols, precision=highest) + bias_cols
    log_decay = jax.nn.log_sigmoid(pre_gate) / normalizer
    q_heads = heads_of(q_rows, DK)
    k_heads = heads_of(k_rows, DK)
    v_heads = heads_of(v_rows, DV)
    decay_heads = heads_of(log_decay, DK)
    running = jnp.cumsum(decay_heads, axis=2)
    ending = running[:, :, -1, :]
    decay_total = jnp.exp(ending)
    local_state = jnp.einsum(
        "shld,shlv->shdv",
        k_heads * jnp.exp(ending[:, :, None, :] - running),
        v_heads,
        precision=highest,
    )
    state_shape = local_state.shape
    states, decays = exchange(
        [
            ("ag", "seq", local_state.astype(bf16).reshape(-1, DV)),
            ("ag", "seq", jnp.broadcast_to(decay_total.reshape(1, -1), (8, decay_total.size))),
        ],
        1,
    )
    decays = decays[:, 0].reshape((n_seq,) + decay_total.shape)
    states = states.reshape((n_seq,) + state_shape)
    start_state = jnp.zeros(state_shape, f32)
    for j in range(n_seq - 1):
        start_state = jnp.where(
            j < seq_pos, decays[j][..., None] * start_state + states[j].astype(f32), start_state
        )

    def mixed(q_part, k_part, v_part, d_part):
        return jax.vmap(jax.vmap(mixer_block))(
            q_part * head_scale, k_part, v_part, d_part, start_state
        )

    (o_heads, end_state), pullback = jax.vjp(mixed, q_heads, k_heads, v_heads, decay_heads)
    gate_heads = heads_of(og_rows, DV)
    scale_three = rms_rows(o_heads)
    gated_norm = o_heads * scale_three * group_gain
    gate_sig = jax.nn.sigmoid(gate_heads)
    gate_act = gate_heads * gate_sig
    mixed_out = rows_of(gated_norm * gate_act).astype(bf16)
    (mix_sum,) = exchange([("ar", "head", spread_head(dot_t(mixed_out, wo_t)))], 2)
    resid = flat_in + mix_sum.reshape(total_rows, width).astype(f32)
    scale_two = rms_rows(resid)
    normed_mid = (resid * scale_two * gain_second).astype(bf16)
    both = product(normed_mid, w_gu)
    gate_pre, up_pre = both[:, :hidden], both[:, hidden:]
    gate_sigma = jax.nn.sigmoid(gate_pre)
    gate_silu = gate_pre * gate_sigma
    mlp_hidden = (gate_silu * up_pre).astype(bf16)
    grad_out_b = flat_cot.astype(bf16)
    d_hidden = product(grad_out_b, wdown_t)
    d_gate_pre = (d_hidden * up_pre * gate_sigma * (1.0 + gate_pre * (1.0 - gate_sigma))).astype(
        bf16
    )
    d_up_pre = (d_hidden * gate_silu).astype(bf16)
    d_both = jnp.concatenate((d_gate_pre, d_up_pre), axis=1)
    sums, mid_two, out_two, both_two, hidden_two = exchange(
        [
            (
                "ar",
                "head",
                spread_head(
                    jnp.concatenate((dot_t(mlp_hidden, wdown_t), dot_t(d_both, w_gu)), axis=0)
                ),
            ),
            ("ag", "dp", normed_mid),
            ("ag", "dp", grad_out_b),
            ("ag", "dp", d_both),
            ("ag", "dp", mlp_hidden),
        ],
        3,
    )
    sums = sums.reshape(2, total_rows, width).astype(f32)
    result = resid + sums[0]
    d_normed_mid = sums[1]
    gain_terms, d_resid_norm = norm_back(resid, scale_two, gain_second, d_normed_mid)
    d_gain_two = jnp.sum(gain_terms, axis=0)
    d_resid = flat_cot + d_resid_norm
    d_resid_b = d_resid.astype(bf16)
    d_mixed = heads_of(product(d_resid_b, wo_t), DV)
    d_norm_out = d_mixed * gate_act
    d_gate_heads = d_mixed * gated_norm * gate_sig * (1.0 + gate_heads * (1.0 - gate_sig))
    d_group = jnp.sum(d_norm_out * o_heads * scale_three, axis=(0, 1, 2))
    group_terms, d_o_heads = norm_back(o_heads, scale_three, group_gain, d_norm_out)
    state_grad = jnp.einsum(
        "shld,shlv->shdv", q_heads * head_scale * jnp.exp(running), d_o_heads, precision=highest
    )
    (grads_in,) = exchange([("ag", "seq", state_grad.astype(bf16).reshape(-1, DV))], 4)
    grads_in = grads_in.reshape((n_seq,) + state_shape)
    later_grad = jnp.zeros(state_shape, f32)
    for j in range(n_seq - 1, 0, -1):
        later_grad = jnp.where(
            j > seq_pos, decays[j][..., None] * later_grad + grads_in[j].astype(f32), later_grad
        )
    d_q, d_k, d_v, d_decay = pullback((d_o_heads, later_grad))
    d_pre = rows_of(d_decay) / normalizer * jax.nn.sigmoid(-pre_gate)
    d_bias = jnp.sum(d_pre, axis=0)
    d_forget = jnp.dot(low_rank.T, d_pre, precision=highest)
    d_low_part = jnp.dot(d_pre, forget_cols.T, precision=highest)
    d_proj = jnp.concatenate(
        (
            rows_of(d_q).astype(bf16),
            rows_of(d_k).astype(bf16),
            rows_of(d_v).astype(bf16),
            rows_of(d_gate_heads).astype(bf16),
        ),
        axis=1,
    )
    d_in_part = jnp.concatenate(
        (dot_t(d_proj, w_attn), d_low_part, jnp.zeros((total_rows, side - rank), f32)), axis=1
    )
    group_rows = d_group.reshape(1, DV)
    if DV < key_cols:
        group_rows = jnp.pad(group_rows, ((0, 0), (0, key_cols - DV)))
    if DV > key_cols:
        group_rows = group_rows.reshape(-1, key_cols)
    used = rank + 1 + group_rows.shape[0]
    small = jnp.concatenate(
        (
            d_forget,
            d_bias[None, :],
            group_rows,
            jnp.zeros((-used % 8, key_cols), f32),
        ),
        axis=0,
    )
    in_sum, small_seq, in_two, proj_two, mixed_two, resid_two = exchange(
        [
            ("ar", "head", spread_head(d_in_part)),
            ("ag", "seq", small),
            ("ag", "dp", normed_in),
            ("ag", "dp", d_proj),
            ("ag", "dp", mixed_out),
            ("ag", "dp", d_resid_b),
        ],
        5,
    )
    in_sum = in_sum.reshape(total_rows, width + side)
    d_low_b = in_sum[:, width : width + rank]
    d_normed_in = in_sum[:, :width].astype(f32) + dot_t(d_low_b, wl_full)
    first_terms, d_in_norm = norm_back(flat_in, scale_one, gain_first, d_normed_in)
    d_gain_one = jnp.sum(first_terms, axis=0)
    grad_in = d_resid + d_in_norm

    def my_rows(array):
        array = array.reshape(n_dp * total_rows, n_seq, n_dp, part_rows)
        array = lax.dynamic_index_in_dim(array, dp_pos, 2, False)
        return array.reshape(n_dp * total_rows, n_seq * part_rows)

    def all_rows(array):
        return array.reshape(n_dp * total_rows, -1)

    grads = jnp.concatenate(
        (
            dot_rows(my_rows(in_two), all_rows(proj_two)).astype(bf16),
            dot_rows(my_rows(resid_two), all_rows(mixed_two)).astype(bf16),
            dot_rows(my_rows(mid_two), all_rows(both_two)).astype(bf16),
            dot_rows(my_rows(out_two), all_rows(hidden_two)).astype(bf16),
        ),
        axis=1,
    ).reshape(n_seq, part_rows, -1)
    tall = jnp.concatenate(
        (
            dot_rows(d_low_b, normed_in),
            d_gain_one[None, :],
            d_gain_two[None, :],
            jnp.zeros((-(rank + 2) % 8, width), f32),
        ),
        axis=0,
    )
    tall = tall.reshape(-1, n_seq, shard_rows).transpose(1, 0, 2)
    grads, tall, small = exchange(
        [
            ("a2a", "seq", grads),
            ("a2a", "seq", tall),
            ("ag", "head", jnp.sum(small_seq, axis=0)),
        ],
        6,
    )
    grads, tall, small = exchange(
        [
            ("ag", "dp", jnp.sum(grads.astype(f32), axis=0)),
            ("ag", "dp", jnp.sum(tall, axis=0)),
            ("ag", "dp", small.reshape(-1, key_cols)),
        ],
        7,
    )
    grads = grads.reshape(shard_rows, -1)
    tall = jnp.sum(tall, axis=0)
    small = jnp.sum(small, axis=0).reshape(n_head, -1, key_cols)
    s_forget = small[:, :rank].transpose(1, 0, 2).reshape(rank, -1)
    s_bias = small[:, rank].reshape(-1)
    s_group = jnp.sum(small[:, rank + 1 : used], axis=0).reshape(-1)[:DV]
    cuts = [key_cols, 2 * key_cols, 2 * key_cols + val_cols, attn_cols, attn_cols + val_cols]
    cuts = cuts + [cuts[-1] + hidden, cuts[-1] + 2 * hidden]
    s_query, s_key, s_value, s_outgate, s_output, s_gate, s_up, s_down = jnp.split(
        grads, cuts, axis=1
    )
    return (
        result.reshape(seqs_here, tok_here, width),
        grad_in.reshape(seqs_here, tok_here, width),
        tall[rank],
        s_query,
        s_key,
        s_value,
        s_outgate,
        tall[:rank].T,
        s_forget,
        s_bias,
        s_group,
        s_output.T,
        tall[rank + 1],
        s_gate,
        s_up,
        s_down.T,
    )


def solution(mesh):
    return jax.shard_map(
        on_device,
        mesh=mesh,
        in_specs=(
            P("dp", "seq", None),
            P("dp", "seq", None),
            P("seq"),
            P("seq", "head"),
            P("seq", "head"),
            P("seq", "head"),
            P("seq", "head"),
            P("seq", None),
            P(),
            P(),
            P(),
            P("head", "seq"),
            P("seq"),
            P("seq", "head"),
            P("seq", "head"),
            P("head", "seq"),
        ),
        out_specs=(
            P("dp", "seq", None),
            P("dp", "seq", None),
            P("seq"),
            P("seq", "head"),
            P("seq", "head"),
            P("seq", "head"),
            P("seq", "head"),
            P("seq", None),
            P(),
            P(),
            P(),
            P("head", "seq"),
            P("seq"),
            P("seq", "head"),
            P("seq", "head"),
            P("head", "seq"),
        ),
        check_vma=False,
    )
```

time: 776 us -> 351 us (0.45)
  waiting for transfers between devices: 447 us -> 0 us
  Pallas kernels: 0 us -> 238 us
  blocking collectives: 214 us -> 0 us
  local copies, waits for them, and re-layouts: 25.7 us -> 41.5 us
  between operations: 16.7 us -> 1.66 us
  matrix products: 40.4 us -> 29.4 us
  other arithmetic: 28.8 us -> 37.9 us
    reduce_scatter x9 -> x0, waiting for transfers between devices: 273 us -> none  [the longest x1 58.4 us: on_device(): lax.psum_scatter(d_up, 'seq', scatter_dimension=0, tiled=True)]
    pallas_call x0 -> x8, Pallas kernels: none -> 238 us  [exchange(): pl.pallas_call(kernel, out_shape=out_shape, in_specs=[vmem] * len(items),...]
    all_gather x11 -> x0, blocking collectives: 149 us -> none  [the longest x3 39 us: entering(): gathered = jax.tree.map(lambda a: lax.all_gather(a, axis), part)]
    psum x5 -> x0, waiting for transfers between devices: 118 us -> none  [the longest x1 44.8 us: on_device(): lax.psum(product(mlp_hidden, wdown_full).astype(jnp.bfloat16), 'head')]
    all_gather x3 -> x0, waiting for transfers between devices: 55 us -> none  [the longest x1 32.5 us: on_device(): lax.all_gather(w_down, 'seq', axis=1, tiled=True)]
    psum x3 -> x0, blocking collectives: 54.5 us -> none  [the longest x1 40.7 us: on_device(): lax.psum((forget_full, bias_full, d_group), ('dp', 'seq', 'head'))]
    dot_general x27 -> x5, matrix products: 34.3 us -> 8.94 us  [product(): return jnp.dot(left, right, preferred_element_type=jnp.float32)]
    dot_general x0 -> x10, matrix products: none -> 13.1 us  [the longest x5 7.46 us: dot_t(): lax.dot_general(left, right, (((1,), (1,)), ((), ())), preferred_element_...]
  transfers between devices with their start and end apart: 17 -> 0, of which waited for: 12 -> 0; matrix products, arithmetic and copies ran while one was open for 4% -> 0% of each run, Pallas kernels for 0% -> 0%
where the time goes in v1:
time: 351 us; the launch traced here: 349 us
  Pallas kernels  238 us (68%)
  local copies, waits for them, and re-layouts  41.5 us (12%)
  other arithmetic  37.9 us (11%)
  matrix products  29.4 us (8%)
    pallas_call x8, Pallas kernels, exchange(): pl.pallas_call(kernel, out_shape=out_shape, in_specs=[vmem] * len(items),...  238 us
    unnamed x98, local copies, waits for them, and re-layouts  14.2 us
    dot_general x5, matrix products, product(): return jnp.dot(left, right, preferred_element_type=jnp.float32)  8.94 us
    dot_general x6, other arithmetic, block_step(): jnp.einsum('id,jd,ijd->ij', query_blk, key_blk, spread, precision=highest)  8.41 us
    dot_general x5, matrix products, dot_t(): lax.dot_general(left, right, (((1,), (1,)), ((), ())), preferred_element_...  7.46 us

profile of v1, /device:TPU:0, one launch (start us, length us, event | category | flops | bytes accessed | tf_op | source)
XLA Modules:
  0.0 349.3 jit_solution(7538878173290669035)
XLA Ops:
  6.7 2.1 concatenate.36.refs_0_
  8.8 69.3 %shard_map.279 = bf16[4,256,3264]{2,1,0:T(8,128)(2,1)} custom-call(bf16[256,3264]{1,0:T(8,128)(2,1)} %concatenate.36.refs_0_), custom_call_target="tpu_custom_call" | custom-call | tf_op jit(solution)/shard_map/pallas_call | solution.py:155
  83.2 1.8 fusion.85
  86.6 29.0 %shard_map.280 = (bf16[4,128,256]{2,1,0:T(8,128)(2,1)}, f32[4,8,128]{2,1,0:T(8,128)}) custom-call(bf16[128,256]{1,0:T(8,128)(2,1)} %convolution_convert_fusion.6.refs_0_, f32[8,128]{1,0:T(8,128)} %broadcast_in_dim.117.refs_1_), custom_call_target="tpu_custom_call" | custom-call | tf_op jit(solution)/shard_map/pallas_call | solution.py:155
  117.9 6.8 %while.40 = (s32[]{:T(128)}, f32[1,1,128,256]{3,2,1,0:T(8,128)S(1)}, f32[2,1,1,64,256]{4,3,2,1,0:T(8,128)S(1)}, f32[2,1,1,128,256]{4,3,2,1,0:T(8,128)S(1)}, f32[...) while((s32[]{:T(128)}, ...), condition=%wide.region_4.5_spmd.clone.clone, body=%wide.region_2.4_spmd.clone.sunk.clone | while | flops 66686976 | bytes 5756017 | solution.py:221
  119.3 1.7 fusion.264
  122.7 1.7 fusion.264
  125.6 2.2 convolution_convert_fusion.4
  127.8 12.6 %shard_map.281 = bf16[4,32,1024]{2,1,0:T(8,128)(2,1)} custom-call(bf16[4,32,1024]{2,1,0:T(8,128)(2,1)} %bitcast.668), custom_call_target="tpu_custom_call" | custom-call | tf_op jit(solution)/shard_map/pallas_call | solution.py:155
  143.6 2.6 fusion.77
  146.3 2.0 multiply_convert_fusion.2
  151.0 17.6 %shard_map.282 = (bf16[4,64,1024]{2,1,0:T(8,128)(2,1)}, bf16[2,128,1024]{2,1,0:T(8,128)(2,1)}, bf16[2,128,1024]{2,1,0:T(8,128)(2,1)}, bf16[2,128,1408]{2,1,0:T(8,128)(2,1)}, bf16[2,128,704]{2,1,0:T(8,128)(2,1)}) custom-call(bf16[4,64,1024]{2,1,0:T(8,128)(2,1)} %bitcast.659, bf16[128,1024]{1,0:T(8,128)(2,1)} %copy-done.13, bf16[128,1024]{1,0:T(8,128)(2,1)} %copy-done.12, ...), custom_call_target="tpu_custom_call" | custom-call | tf_op jit(solution)/shard_map/pallas_call | solution.py:155
  174.2 10.7 %shard_map.283 = bf16[4,128,256]{2,1,0:T(8,128)(2,1)} custom-call(bf16[128,256]{1,0:T(8,128)(2,1)} %convolution_convert_fusion.5.refs_0_), custom_call_target="tpu_custom_call" | custom-call | tf_op jit(solution)/shard_map/pallas_call | solution.py:155
  186.1 14.6 %while.41 = (s32[]{:T(128)}, f32[1,1,128,256]{2,3,1,0:T(8,128)S(1)}, f32[2,1,1,64,128]{4,3,2,1,0:T(8,128)S(1)}, bf16[2,1,1,64,128]{4,3,2,1,0:T(8,128)(2,1)S(1)},...) while((s32[]{:T(128)}, ...), condition=%wide.region_16.17_spmd.clone.clone, body=%wide.region_9.16_spmd.clone.sunk.clone | while | flops 141848576 | bytes 3989677 | solution.py:221
  190.5 2.3 fusion.285
  197.7 2.3 fusion.285
  200.7 2.0 fusion.87
  205.6 16.4 %shard_map.284 = (bf16[4,32,1152]{2,1,0:T(8,128)(2,1)}, f32[4,24,128]{2,1,0:T(8,128)}, bf16[2,128,1024]{2,1,0:T(8,128)(2,1)}, bf16[2,128,768]{2,1,0:T(8,128)(2,1...) custom-call(bf16[4,32,1152]{2,1,0:T(8,128)(2,1)} %concatenate.42.refs_0_, ...), custom_call_target="tpu_custom_call" | custom-call | tf_op jit(solution)/shard_map/pallas_call | solution.py:155
  222.1 1.5 fusion.110
  226.9 1.4 convolution_convert_fusion.2
  229.0 1.7 convolution_convert_fusion
  230.8 2.2 reshape.1155
  233.0 2.4 constant_dynamic-slice_fusion.3
  237.0 2.2 reshape.1152
  239.2 2.4 constant_dynamic-slice_fusion.4
  244.2 1.8 pad_maximum_fusion
  248.7 75.5 %shard_map.285 = (bf16[4,128,3136]{2,1,0:T(8,128)(2,1)}, f32[4,24,256]{2,1,0:T(8,128)}, f32[4,24,128]{2,1,0:T(8,128)}) custom-call(bf16[4,128,3136]{2,1,0:T(8,128)(2,1)} %bitcast.633, f32[4,24,256]{2,1,0:T(8,128)} %maximum_bitcast_fusion.refs_1_, f32[24,128]{1,0:T(8,128)} %reduce_sum.206.refs_2_), custom_call_target="tpu_custom_call" | custom-call | tf_op jit(solution)/shard_map/pallas_call | solution.py:155
  324.2 3.7 %convert_reduce_fusion.refs_0_ = f32[128,3136]{1,0:T(8,128)} fusion(bf16[4,128,3136]{2,1,0:T(8,128)(2,1)} %get-tuple-element.368), kind=kLoop, calls=%fused_computation.110 | loop fusion | flops 2809856 | bytes 4816896 | tf_op jit(solution)/shard_map/reduce_sum | solution.py:499
  328.6 7.1 %shard_map.286 = (f32[2,128,3136]{2,1,0:T(8,128)}, f32[2,24,256]{2,1,0:T(8,128)}, f32[2,96,128]{2,1,0:T(8,128)}) custom-call(f32[128,3136]{1,0:T(8,128)} %convert_reduce_fusion.refs_0_, f32[24,256]{1,0:T(8,128)} %reduce_sum.208.refs_1_, f32[96,128]{1,0:T(8,128)} %bitcast.694), custom_call_target="tpu_custom_call" | custom-call | tf_op jit(solution)/shard_map/pallas_call | solution.py:155
  337.1 1.7 fusion.158
  338.8 2.0 fusion.157
  344.0 1.9 fusion.156
  (252 shorter events, 63.3 us)
Async XLA Ops:
  0.6 82.0 %copy-start = (f32[16,512]{1,0:T(8,128)S(1)}, f32[16,512]{1,0:T(8,128)}, u32[]{:S(2)}) copy-start(f32[16,512]{1,0:T(8,128)} %param.28) | copy-start | bytes 98308
  0.7 6.0 %copy-start.27 = (bf16[256,128]{1,0:T(8,128)(2,1)S(1)}, bf16[256,128]{1,0:T(8,128)(2,1)}, u32[]{:S(2)}) copy-start(bf16[256,128]{1,0:T(8,128)(2,1)} %param.23) | copy-start | bytes 196612
  0.7 6.0 %copy-start.28 = (bf16[256,128]{1,0:T(8,128)(2,1)S(1)}, bf16[256,128]{1,0:T(8,128)(2,1)}, u32[]{:S(2)}) copy-start(bf16[256,128]{1,0:T(8,128)(2,1)} %param.24) | copy-start | bytes 196612
  0.7 6.0 %copy-start.22 = (bf16[256,256]{1,0:T(8,128)(2,1)S(1)}, bf16[256,256]{1,0:T(8,128)(2,1)}, u32[]{:S(2)}) copy-start(bf16[256,256]{1,0:T(8,128)(2,1)} %param.25) | copy-start | bytes 393220
  0.7 6.0 %copy-start.23 = (bf16[256,256]{1,0:T(8,128)(2,1)S(1)}, bf16[256,256]{1,0:T(8,128)(2,1)}, u32[]{:S(2)}) copy-start(bf16[256,256]{1,0:T(8,128)(2,1)} %param.26) | copy-start | bytes 393220
  0.7 5.8 %copy-start.20 = (bf16[704,256]{1,0:T(8,128)(2,1)S(1)}, bf16[704,256]{1,0:T(8,128)(2,1)}, u32[]{:S(2)}) copy-start(bf16[704,256]{1,0:T(8,128)(2,1)} %param.35) | copy-start | bytes 1081348
  78.2 1.7 copy-start.1
  80.6 37.3 %copy-start.3 = (bf16[128,1024]{1,0:T(8,128)(2,1)}, bf16[128,1024]{1,0:T(8,128)(2,1)S(1)}, u32[]{:S(2)}) copy-start(bf16[128,1024]{1,0:T(8,128)(2,1)S(1)} %fusion.103.refs_2_) | copy-start | bytes 786436
  83.2 33.6 %copy-start.15 = (f32[1,1,128,128]{3,2,1,0:T(8,128)}, f32[1,1,128,128]{3,2,1,0:T(8,128)S(1)}, u32[]{:S(2)}) copy-start(f32[1,1,128,128]{3,2,1,0:T(8,128)S(1)} %reduce_window_sum.52) | copy-start | bytes 196612
  85.0 39.9 %copy-start.7 = (f32[128,768]{1,0:T(8,128)}, f32[128,768]{1,0:T(8,128)S(1)}, u32[]{:S(2)}) copy-start(f32[128,768]{1,0:T(8,128)S(1)} %fusion.85) | copy-start | bytes 1179652
  117.9 7.5 %copy-start.34 = (f32[256]{0:T(256)S(1)}, f32[256]{0:T(256)}, u32[]{:S(2)}) copy-start(f32[256]{0:T(256)} %param.30) | copy-start | bytes 3076
  125.5 20.7 %copy-start.30 = (f32[128]{0:T(128)}, f32[128]{0:T(128)S(1)}, u32[]{:S(2)}) copy-start(f32[128]{0:T(128)S(1)} %rsqrt.38) | copy-start | bytes 1540
  125.5 16.4 %copy-start.17 = (bf16[128,256]{1,0:T(8,128)(2,1)}, bf16[128,256]{1,0:T(8,128)(2,1)S(1)}, u32[]{:S(2)}) copy-start(bf16[128,256]{1,0:T(8,128)(2,1)S(1)} %multiply_convert_fusion.5.refs_4_) | copy-start | bytes 196612
  125.6 22.8 %slice-start = ((s8[6815744]{0:T(1024)(128)(4,1)}), s8[2621440]{0:T(1024)(128)(4,1)S(1)}, s32[]{:S(2)}) async-start(s8[6815744]{0:T(1024)(128)(4,1)} %bitcast.645), calls=%async_computation | async-start | bytes 5242880
  142.5 3.7 %copy-start.4 = (f32[1,128,1024]{2,1,0:T(8,128)S(1)}, f32[1,128,1024]{2,1,0:T(8,128)}, u32[]{:S(2)}) copy-start(f32[1,128,1024]{2,1,0:T(8,128)} %param.21) | copy-start | bytes 1572868
  143.6 2.6 copy-start.13
  143.6 4.8 %slice-start.1 = ((s8[6815744]{0:T(1024)(128)(4,1)}), s8[4194304]{0:T(1024)(128)(4,1)S(1)}, s32[]{:S(2)}) async-start(s8[6815744]{0:T(1024)(128)(4,1)} %bitcast.645), calls=%async_computation.1 | async-start | bytes 8388608
  146.3 2.0 copy-start.12
  148.3 1.3 copy-start.21
  151.0 18.7 %copy-start.2 = (bf16[4,32,1024]{2,1,0:T(8,128)(2,1)S(1)}, bf16[4,32,1024]{2,1,0:T(8,128)(2,1)}, u32[]{:S(2)}) copy-start(bf16[4,32,1024]{2,1,0:T(8,128)(2,1)} %shard_map.281) | copy-start | bytes 786436
  168.6 2.1 copy-start.33
  170.9 2.3 copy-start.16
  171.2 14.9 %copy-start.14 = (bf16[128,1024]{1,0:T(8,128)(2,1)}, bf16[128,1024]{1,0:T(8,128)(2,1)S(1)}, u32[]{:S(2)}) copy-start(bf16[128,1024]{1,0:T(8,128)(2,1)S(1)} %get-tuple-element.577.refs_5_) | copy-start | bytes 786436
  171.2 13.7 %copy-start.36 = (f32[128]{0:T(128)S(1)}, f32[128]{0:T(128)}, u32[]{:S(2)}) copy-start(f32[128]{0:T(128)} %get-tuple-element.611) | copy-start | bytes 1540
  171.2 14.9 %copy-start.6 = (f32[2,1,1,128,256]{4,3,2,1,0:T(8,128)S(1)}, f32[2,1,1,128,256]{4,3,2,1,0:T(8,128)}, u32[]{:S(2)}) copy-start(f32[2,1,1,128,256]{4,3,2,1,0:T(8,128)} %copy-done.5) | copy-start | bytes 786436
  202.8 20.8 %copy-start.37 = (f32[128]{0:T(128)S(1)}, f32[128]{0:T(128)}, u32[]{:S(2)}) copy-start(f32[128]{0:T(128)} %get-tuple-element.615) | copy-start | bytes 1540
  205.6 18.9 %copy-start.19 = (bf16[2,128,1024]{2,1,0:T(8,128)(2,1)S(1)}, bf16[2,128,1024]{2,1,0:T(8,128)(2,1)}, u32[]{:S(2)}) copy-start(bf16[2,128,1024]{2,1,0:T(8,128)(2,1)} %get-tuple-element.365) | copy-start | bytes 1572868
  222.0 2.9 copy-start.18
  229.0 7.5 %copy-start.24 = (bf16[2,128,256]{2,1,0:T(8,128)(2,1)S(1)}, bf16[2,128,256]{2,1,0:T(8,128)(2,1)}, u32[]{:S(2)}) copy-start(bf16[2,128,256]{2,1,0:T(8,128)(2,1)} %get-tuple-element.362) | copy-start | bytes 393220
  244.2 3.9 %copy-start.29 = (f32[4,24,128]{2,1,0:T(8,128)S(1)}, f32[4,24,128]{2,1,0:T(8,128)}, u32[]{:S(2)}) copy-start(f32[4,24,128]{2,1,0:T(8,128)} %get-tuple-element.367) | copy-start | bytes 147460
  324.2 3.7 %copy-start.26 = (f32[4,24,256]{2,1,0:T(8,128)S(1)}, f32[4,24,256]{2,1,0:T(8,128)}, u32[]{:S(2)}) copy-start(f32[4,24,256]{2,1,0:T(8,128)} %get-tuple-element.369) | copy-start | bytes 294916
  335.7 5.7 %copy-start.25 = (f32[2,96,128]{2,1,0:T(8,128)S(1)}, f32[2,96,128]{2,1,0:T(8,128)}, u32[]{:S(2)}) copy-start(f32[2,96,128]{2,1,0:T(8,128)} %get-tuple-element.373) | copy-start | bytes 294916
  (9 other events, 8.3 us)

commit v2 on v1

--- a/solution.py
+++ b/solution.py
@@ -16,138 +16,338 @@
 
 
 def exchange(items, cid):
-    axes = []
+    groups = []
     for kind, axis, _ in items:
-        for name in axis if kind == "wg" else (axis,):
-            if name not in axes:
-                axes.append(name)
-    size = {name: lax.axis_size(name) for name in axes}
+        for name in axis if kind in ("wg", "rs") else (axis,):
+            if name not in groups:
+                groups.append(name)
+    names = []
+    for group in groups:
+        for name in group if isinstance(group, tuple) else (group,):
+            if name not in names:
+                names.append(name)
+    size = {name: lax.axis_size(name) for name in names}
+    for group in groups:
+        if isinstance(group, tuple):
+            size[group] = size[group[0]] * size[group[1]]
     out_shape, scratch = [], []
+    dma = pltpu.SemaphoreType.DMA
     for kind, axis, arr in items:
-        if kind == "ag":
-            out_shape.append(jax.ShapeDtypeStruct((size[axis],) + arr.shape, arr.dtype))
-        elif kind == "wg":
-            out_shape.append(jax.ShapeDtypeStruct((size[axis[0]],) + arr.shape, arr.dtype))
+        if kind in ("wg", "rs"):
+            n, m = size[axis[0]], size[axis[1]]
+            scratch += [dma((2, 2, n)), dma((2, 2, n, m))]
+            if kind == "wg":
+                out_shape.append(jax.ShapeDtypeStruct((n,) + arr.shape, arr.dtype))
+                scratch.append(dma)
+            else:
+                out_shape.append(jax.ShapeDtypeStruct((m,) + arr.shape[1:], jnp.float32))
+                scratch.append(pltpu.VMEM((2,) + arr.shape, arr.dtype))
+                scratch.append(pltpu.VMEM((2,) + arr.shape, arr.dtype))
+            continue
+        n = size[axis]
+        scratch.append(dma((2, n)))
+        if kind == "ar":
+            out_shape.append(jax.ShapeDtypeStruct(arr.shape, arr.dtype))
+            scratch += [dma((2, n)), pltpu.VMEM(arr.shape, arr.dtype)]
         else:
-            out_shape.append(jax.ShapeDtypeStruct(arr.shape, arr.dtype))
-        n = size[axis[0]] if kind == "wg" else size[axis]
-        scratch.append(pltpu.SemaphoreType.DMA((2, n)))
-        if kind == "ar":
-            scratch.append(pltpu.SemaphoreType.DMA((2, n)))
-            scratch.append(pltpu.VMEM(arr.shape, arr.dtype))
-        elif kind == "wg":
-            scratch.append(pltpu.SemaphoreType.DMA((2, n, size[axis[1]])))
-        if kind != "ar":
-            scratch.append(pltpu.SemaphoreType.DMA)
+            inner = arr.shape if kind == "ag" else arr.shape[1:]
+            out_shape.append(jax.ShapeDtypeStruct((n,) + inner, arr.dtype))
+            scratch.append(dma)
 
     def kernel(*refs):
         count = len(items)
         ins, outs, rest = refs[:count], refs[count : 2 * count], list(refs[2 * count :])
-        me = {name: lax.axis_index(name) for name in axes}
+        me = {name: lax.axis_index(name) for name in names}
+        for group in groups:
+            if isinstance(group, tuple):
+                me[group] = me[group[0]] * size[group[1]] + me[group[1]]
+
+        def device(group, place):
+            if isinstance(group, tuple):
+                return {
+                    group[0]: place // size[group[1]],
+                    group[1]: lax.rem(place, size[group[1]]),
+                }
+            return {group: place}
+
         barrier = pltpu.get_barrier_semaphore()
-        for name in axes:
-            for k in range(1, size[name]):
-                peer = lax.rem(me[name] + k, size[name])
+        for group in groups:
+            for k in range(1, size[group]):
                 pl.semaphore_signal(
-                    barrier, inc=1, device_id={name: peer}, device_id_type=pl.DeviceIdType.MESH
+                    barrier,
+                    inc=1,
+                    device_id=device(group, lax.rem(me[group] + k, size[group])),
+                    device_id_type=pl.DeviceIdType.MESH,
                 )
-        pl.semaphore_wait(barrier, sum(size[name] - 1 for name in axes))
-
-        def remote(source, target, sems, k, name, peer):
+        pl.semaphore_wait(barrier, sum(size[group] - 1 for group in groups))
+
+        def remote(source, target, send, recv, group, place):
             return pltpu.make_async_remote_copy(
                 src_ref=source,
                 dst_ref=target,
-                send_sem=sems.at[(0,) + k],
-                recv_sem=sems.at[(1,) + k],
-                device_id={name: peer},
+                send_sem=send,
+                recv_sem=recv,
+                device_id=device(group, place),
                 device_id_type=pl.DeviceIdType.MESH,
             )
 
-        waits, later = [], []
+        waits, chains, sums = [], [], []
+
+        def chain_gather(src, dst, sems, sems_two, local, axis, arr):
+            name, other = axis
+            n, here, m, place = size[name], me[name], size[other], me[other]
+            part = arr.shape[0] // m
+            rows = pl.ds(pl.multiple_of(place * part, part), part)
+            own = pltpu.make_async_copy(src, dst.at[here], local)
+            own.start()
+            waits.append(own.wait)
+
+            def hop(way, step, source, index):
+                to = here + 1 if way == 0 else here - 1
+                return remote(
+                    source,
+                    dst.at[index, rows],
+                    sems.at[way, 0, step],
+                    sems.at[way, 1, step],
+                    name,
+                    to,
+                )
+
+            def guarded(ok, call):
+                waits.append(lambda: pl.when(ok)(call))
+
+            open_ends = (here < n - 1, here > 0)
+            for way in range(2):
+                @pl.when(open_ends[way])
+                def _():
+                    hop(way, 0, src.at[rows], here).start()
+
+                guarded(
+                    open_ends[way],
+                    lambda way=way: hop(way, 0, src.at[rows], here).wait_send(),
+                )
+
+            def advance(step):
+                for way in range(2):
+                    came = here - 1 - step if way == 0 else here + 1 + step
+                    ok = came >= 0 if way == 0 else came < n
+                    on = jnp.logical_and(ok, open_ends[way])
+
+                    def partners(way=way, came=came):
+                        for j in range(1, m):
+                            to = lax.rem(place + j, m)
+                            whose = lax.rem(place + m - j, m)
+                            piece = dst.at[came, rows]
+                            theirs = dst.at[came, pl.ds(pl.multiple_of(whose * part, part), part)]
+                            send, recv = sems_two.at[way, 0, step, j], sems_two.at[way, 1, step, j]
+                            yield (
+                                remote(piece, piece, send, recv, other, to),
+                                remote(theirs, theirs, send, recv, other, to),
+                            )
+
+                    @pl.when(ok)
+                    def _():
+                        hop(way, step, dst.at[came, rows], came).wait_recv()
+
+                    if step + 1 < n - 1:
+                        @pl.when(on)
+                        def _():
+                            hop(way, step + 1, dst.at[came, rows], came).start()
+
+                        guarded(
+                            on,
+                            lambda way=way, came=came: hop(
+                                way, step + 1, dst.at[came, rows], came
+                            ).wait_send(),
+                        )
+
+                    @pl.when(ok)
+                    def _():
+                        for copy, _ in partners():
+                            copy.start()
+
+                    def finish(partners=partners):
+                        for copy, arrival in partners():
+                            copy.wait_send()
+                            arrival.wait_recv()
+
+                    guarded(ok, finish)
+
+            chains.append((n - 1, advance, lambda: None))
+
+        def chain_sum(src, dst, sems, sems_two, land, held, axis, arr):
+            name, other = axis
+            n, here, m, place = size[name], me[name], size[other], me[other]
+            tall = 16 if arr.shape[1] % 16 == 0 else arr.shape[1]
+            turns = arr.shape[1] // tall
+
+            def by_rows(call):
+                def one(turn, carry):
+                    call(pl.ds(pl.multiple_of(turn * tall, tall), tall))
+                    return carry
+
+                lax.fori_loop(0, turns, one, 0)
+
+            def hop(way, step, source, index):
+                to = here + 1 if way == 0 else here - 1
+                return remote(
+                    source,
+                    land.at[way, index],
+                    sems.at[way, 0, step],
+                    sems.at[way, 1, step],
+                    name,
+                    to,
+                )
+
+            def guarded(ok, call):
+                waits.append(lambda: pl.when(ok)(call))
+
+            firsts = (here == 0, here == n - 1)
+
+            def advance(step):
+                for way in range(2):
+                    goal = n - 1 - step if way == 0 else step
+                    passing = here < goal if way == 0 else here > goal
+                    inner = jnp.logical_and(passing, jnp.logical_not(firsts[way]))
+                    first = jnp.logical_and(passing, firsts[way])
+
+                    @pl.when(first)
+                    def _():
+                        hop(way, step, src.at[goal], goal).start()
+
+                    guarded(
+                        first,
+                        lambda way=way, goal=goal: hop(way, step, src.at[goal], goal).wait_send(),
+                    )
+
+                    @pl.when(inner)
+                    def _():
+                        hop(way, step, land.at[way, goal], goal).wait_recv()
+
+                        def add(rows):
+                            held[way, goal, rows] = (
+                                land[way, goal, rows].astype(jnp.float32)
+                                + src[goal, rows].astype(jnp.float32)
+                            ).astype(held.dtype)
+
+                        by_rows(add)
+                        hop(way, step, held.at[way, goal], goal).start()
+
+                    guarded(
+                        inner,
+                        lambda way=way, goal=goal: hop(
+                            way, step, held.at[way, goal], goal
+                        ).wait_send(),
+                    )
+
+            def partners():
+                for j in range(1, m):
+                    to = lax.rem(place + j, m)
+                    whose = lax.rem(place + m - j, m)
+                    send, recv = sems_two.at[0, 0, 0, j], sems_two.at[0, 1, 0, j]
+                    yield (
+                        remote(dst.at[place], dst.at[place], send, recv, other, to),
+                        remote(dst.at[whose], dst.at[whose], send, recv, other, to),
+                    )
+
+            def close():
+                def start(rows):
+                    dst[place, rows] = src[here, rows].astype(jnp.float32)
+
+                by_rows(start)
+                for way in range(2):
+                    step = n - 1 - here if way == 0 else here
+
+                    @pl.when(jnp.logical_not(firsts[way]))
+                    def _():
+                        hop(way, step, land.at[way, here], here).wait_recv()
+
+                        def add(rows):
+                            dst[place, rows] = dst[place, rows] + land[way, here, rows].astype(
+                                jnp.float32
+                            )
+
+                        by_rows(add)
+
+                for copy, _ in partners():
+                    copy.start()
+                for copy, arrival in partners():
+                    waits.append(copy.wait_send)
+                    waits.append(arrival.wait_recv)
+
+            chains.append((n, advance, close))
+
         for (kind, axis, arr), src, dst in zip(items, ins, outs):
+            if kind in ("wg", "rs"):
+                extra = [rest.pop(0) for _ in range(3 if kind == "wg" else 4)]
+                (chain_gather if kind == "wg" else chain_sum)(src, dst, *extra, axis, arr)
+                continue
             sems = rest.pop(0)
-            name = axis[0] if kind == "wg" else axis
-            n, here = size[name], me[name]
+            n, here = size[axis], me[axis]
             if kind == "ar":
                 sems_two, land = rest.pop(0), rest.pop(0)
                 sent = []
                 for k in range(1, n):
                     peer = lax.rem(here + k, n)
                     came = lax.rem(here + n - k, n)
-                    copy = remote(src.at[peer], land.at[here], sems, (k,), name, peer)
+                    pair = sems.at[0, k], sems.at[1, k]
+                    copy = remote(src.at[peer], land.at[here], *pair, axis, peer)
                     copy.start()
-                    sent.append((copy, remote(land.at[came], land.at[came], sems, (k,), name, peer)))
-                later.append(("ar", src, dst, land, sems_two, name, n, here, sent))
+                    sent.append((copy, remote(land.at[came], land.at[came], *pair, axis, peer)))
+                sums.append((src, dst, land, sems_two, axis, n, here, sent))
                 continue
-            if kind == "wg":
-                sems_two = rest.pop(0)
             local = rest.pop(0)
-            if kind == "wg":
-                other = axis[1]
-                part = arr.shape[0] // size[other]
-                rows = pl.ds(pl.multiple_of(me[other] * part, part), part)
-                own = pltpu.make_async_copy(src, dst.at[here], local)
-                own.start()
-                waits.append(own.wait)
-                sent = []
-                for k in range(1, n):
-                    peer = lax.rem(here + k, n)
-                    came = lax.rem(here + n - k, n)
-                    copy = remote(src.at[rows], dst.at[here, rows], sems, (k,), name, peer)
-                    copy.start()
-                    arrived = dst.at[came, rows]
-                    sent.append((copy, remote(arrived, arrived, sems, (k,), name, peer), came))
-                later.append(("wg", dst, sems_two, other, part, rows, sent))
-                continue
-            piece = src if kind == "ag" else src.at[here]
-            own = pltpu.make_async_copy(piece, dst.at[here], local)
+
+            def piece(place):
+                if kind == "ag":
+                    return src
+                if isinstance(axis, tuple):
+                    return src.at[place // size[axis[1]]]
+                return src.at[place]
+
+            own = pltpu.make_async_copy(piece(here), dst.at[here], local)
             own.start()
             waits.append(own.wait)
             for k in range(1, n):
                 peer = lax.rem(here + k, n)
                 came = lax.rem(here + n - k, n)
-                piece = src if kind == "ag" else src.at[peer]
-                copy = remote(piece, dst.at[here], sems, (k,), name, peer)
+                pair = sems.at[0, k], sems.at[1, k]
+                copy = remote(piece(peer), dst.at[here], *pair, axis, peer)
                 copy.start()
                 waits.append(copy.wait_send)
-                waits.append(remote(dst.at[came], dst.at[came], sems, (k,), name, peer).wait_recv)
-        for entry in later:
-            if entry[0] == "ar":
-                _, src, dst, land, sems_two, name, n, here, sent = entry
+                waits.append(remote(dst.at[came], dst.at[came], *pair, axis, peer).wait_recv)
+
+        def finish_sums():
+            for src, dst, land, sems_two, axis, n, here, sent in sums:
                 total = src[here].astype(jnp.float32)
                 for k, (copy, arrival) in enumerate(sent, 1):
                     arrival.wait_recv()
-                    came = lax.rem(here + n - k, n)
-                    total = total + land[came].astype(jnp.float32)
+                    total = total + land[lax.rem(here + n - k, n)].astype(jnp.float32)
                 dst[here] = total.astype(dst.dtype)
                 for k in range(1, n):
                     peer = lax.rem(here + k, n)
                     came = lax.rem(here + n - k, n)
-                    copy = remote(dst.at[here], dst.at[here], sems_two, (k,), name, peer)
+                    pair = sems_two.at[0, k], sems_two.at[1, k]
+                    copy = remote(dst.at[here], dst.at[here], *pair, axis, peer)
                     copy.start()
                     waits.append(copy.wait_send)
                     waits.append(
-                        remote(dst.at[came], dst.at[came], sems_two, (k,), name, peer).wait_recv
+                        remote(dst.at[came], dst.at[came], *pair, axis, peer).wait_recv
                     )
                 for copy, _ in sent:
                     waits.append(copy.wait_send)
-            else:
-                _, dst, sems_two, other, part, rows, sent = entry
-                m, place = size[other], me[other]
-                for k, (copy, arrival, came) in enumerate(sent, 1):
-                    arrival.wait_recv()
-                    waits.append(copy.wait_send)
-                    for j in range(1, m):
-                        partner = lax.rem(place + j, m)
-                        whose = lax.rem(place + m - j, m)
-                        theirs = dst.at[came, pl.ds(pl.multiple_of(whose * part, part), part)]
-                        piece = dst.at[came, rows]
-                        onward = remote(piece, piece, sems_two, (k, j), other, partner)
-                        onward.start()
-                        waits.append(onward.wait_send)
-                        waits.append(
-                            remote(theirs, theirs, sems_two, (k, j), other, partner).wait_recv
-                        )
+
+        steps = max([entry[0] for entry in chains], default=0)
+        for step in range(steps):
+            if step == 1:
+                finish_sums()
+            for last, advance, _ in chains:
+                if step < last:
+                    advance(step)
+        if steps < 2:
+            finish_sums()
+        for _, _, close in chains:
+            close()
         for wait in waits:
             wait()
 
@@ -248,11 +448,7 @@
     total_rows = seqs_here * tok_here
     bf16, f32 = jnp.bfloat16, jnp.float32
     n_seq, n_head, n_dp = lax.axis_size("seq"), lax.axis_size("head"), lax.axis_size("dp")
-    seq_pos, head_pos, dp_pos = (
-        lax.axis_index("seq"),
-        lax.axis_index("head"),
-        lax.axis_index("dp"),
-    )
+    seq_pos, head_pos = lax.axis_index("seq"), lax.axis_index("head")
     shard_rows = w_query.shape[0]
     part_rows = shard_rows // n_dp
     key_cols, val_cols, hidden = w_query.shape[1], w_value.shape[1], w_gate.shape[1]
@@ -271,12 +467,10 @@
             mlp_gain[:, None],
             jnp.zeros((shard_rows, side - rank - 2), bf16),
             w_output.T,
-            w_gate,
-            w_up,
-            w_down.T,
         ),
         axis=1,
     )
+    packed_mlp = jnp.concatenate((w_gate, w_up, w_down.T), axis=1)
     (weights,) = exchange([("wg", ("seq", "dp"), packed)], 0)
     weights = weights.reshape(width, -1)
     attn_cols = 2 * key_cols + 2 * val_cols
@@ -287,9 +481,6 @@
     gain_second = w_low[:, rank + 1].astype(f32)
     at = attn_cols + side
     wo_t = weights[:, at : at + val_cols]
-    at = at + val_cols
-    w_gu = weights[:, at : at + 2 * hidden]
-    wdown_t = weights[:, at + 2 * hidden :]
     forget_cols = lax.dynamic_slice_in_dim(w_forget, head_pos * key_cols, key_cols, 1)
     bias_cols = lax.dynamic_slice_in_dim(forget_bias, head_pos * key_cols, key_cols, 0)
 
@@ -301,6 +492,16 @@
 
     def spread_head(array):
         return array.astype(bf16).reshape(n_head, array.shape[0] // n_head, array.shape[1])
+
+    def by_part(array):
+        array = array.reshape(total_rows, n_seq, n_dp, part_rows)
+        return array.transpose(2, 0, 1, 3).reshape(n_dp, total_rows, n_seq * part_rows)
+
+    def all_rows(array):
+        return array.reshape(n_dp * total_rows, -1)
+
+    def grad_of(left, right):
+        return dot_rows(all_rows(left), all_rows(right)).astype(bf16)
 
     flat_in = x_in.reshape(total_rows, width)
     flat_cot = cotangent.reshape(total_rows, width)
@@ -355,7 +556,16 @@
     gate_sig = jax.nn.sigmoid(gate_heads)
     gate_act = gate_heads * gate_sig
     mixed_out = rows_of(gated_norm * gate_act).astype(bf16)
-    (mix_sum,) = exchange([("ar", "head", spread_head(dot_t(mixed_out, wo_t)))], 2)
+    mix_sum, weights_mlp = exchange(
+        [
+            ("ar", "head", spread_head(dot_t(mixed_out, wo_t))),
+            ("wg", ("seq", "dp"), packed_mlp),
+        ],
+        2,
+    )
+    weights_mlp = weights_mlp.reshape(width, -1)
+    w_gu = weights_mlp[:, : 2 * hidden]
+    wdown_t = weights_mlp[:, 2 * hidden :]
     resid = flat_in + mix_sum.reshape(total_rows, width).astype(f32)
     scale_two = rms_rows(resid)
     normed_mid = (resid * scale_two * gain_second).astype(bf16)
@@ -380,8 +590,8 @@
                     jnp.concatenate((dot_t(mlp_hidden, wdown_t), dot_t(d_both, w_gu)), axis=0)
                 ),
             ),
-            ("ag", "dp", normed_mid),
-            ("ag", "dp", grad_out_b),
+            ("a2a", "dp", by_part(normed_mid)),
+            ("a2a", "dp", by_part(grad_out_b)),
             ("ag", "dp", d_both),
             ("ag", "dp", mlp_hidden),
         ],
@@ -402,7 +612,22 @@
     state_grad = jnp.einsum(
         "shld,shlv->shdv", q_heads * head_scale * jnp.exp(running), d_o_heads, precision=highest
     )
-    (grads_in,) = exchange([("ag", "seq", state_grad.astype(bf16).reshape(-1, DV))], 4)
+    grads_in, mixed_two, resid_two = exchange(
+        [
+            ("ag", "seq", state_grad.astype(bf16).reshape(-1, DV)),
+            ("ag", "dp", mixed_out),
+            ("a2a", "dp", by_part(d_resid_b)),
+        ],
+        4,
+    )
+    grads_late = jnp.concatenate(
+        (
+            grad_of(resid_two, mixed_two),
+            grad_of(mid_two, both_two),
+            grad_of(out_two, hidden_two),
+        ),
+        axis=1,
+    ).reshape(n_seq, part_rows, -1)
     grads_in = grads_in.reshape((n_seq,) + state_shape)
     later_grad = jnp.zeros(state_shape, f32)
     for j in range(n_seq - 1, 0, -1):
@@ -441,14 +666,13 @@
         ),
         axis=0,
     )
-    in_sum, small_seq, in_two, proj_two, mixed_two, resid_two = exchange(
+    grads_late, in_sum, small_all, in_two, proj_two = exchange(
         [
+            ("rs", ("seq", "dp"), grads_late),
             ("ar", "head", spread_head(d_in_part)),
-            ("ag", "seq", small),
-            ("ag", "dp", normed_in),
+            ("ag", ("seq", "dp"), small),
+            ("a2a", "dp", by_part(normed_in)),
             ("ag", "dp", d_proj),
-            ("ag", "dp", mixed_out),
-            ("ag", "dp", d_resid_b),
         ],
         5,
     )
@@ -459,23 +683,7 @@
     d_gain_one = jnp.sum(first_terms, axis=0)
     grad_in = d_resid + d_in_norm
 
-    def my_rows(array):
-        array = array.reshape(n_dp * total_rows, n_seq, n_dp, part_rows)
-        array = lax.dynamic_index_in_dim(array, dp_pos, 2, False)
-        return array.reshape(n_dp * total_rows, n_seq * part_rows)
-
-    def all_rows(array):
-        return array.reshape(n_dp * total_rows, -1)
-
-    grads = jnp.concatenate(
-        (
-            dot_rows(my_rows(in_two), all_rows(proj_two)).astype(bf16),
-            dot_rows(my_rows(resid_two), all_rows(mixed_two)).astype(bf16),
-            dot_rows(my_rows(mid_two), all_rows(both_two)).astype(bf16),
-            dot_rows(my_rows(out_two), all_rows(hidden_two)).astype(bf16),
-        ),
-        axis=1,
-    ).reshape(n_seq, part_rows, -1)
+    grads_attn = grad_of(in_two, proj_two).reshape(n_seq, part_rows, -1)
     tall = jnp.concatenate(
         (
             dot_rows(d_low_b, normed_in),
@@ -486,32 +694,25 @@
         axis=0,
     )
     tall = tall.reshape(-1, n_seq, shard_rows).transpose(1, 0, 2)
-    grads, tall, small = exchange(
+    grads_attn, tall, small = exchange(
         [
-            ("a2a", "seq", grads),
-            ("a2a", "seq", tall),
-            ("ag", "head", jnp.sum(small_seq, axis=0)),
+            ("rs", ("seq", "dp"), grads_attn),
+            ("a2a", ("seq", "dp"), tall),
+            ("ag", "head", jnp.sum(small_all, axis=0)),
         ],
         6,
     )
-    grads, tall, small = exchange(
-        [
-            ("ag", "dp", jnp.sum(grads.astype(f32), axis=0)),
-            ("ag", "dp", jnp.sum(tall, axis=0)),
-            ("ag", "dp", small.reshape(-1, key_cols)),
-        ],
-        7,
-    )
-    grads = grads.reshape(shard_rows, -1)
+    grads_attn = grads_attn.reshape(shard_rows, -1)
+    grads_late = grads_late.reshape(shard_rows, -1)
     tall = jnp.sum(tall, axis=0)
-    small = jnp.sum(small, axis=0).reshape(n_head, -1, key_cols)
     s_forget = small[:, :rank].transpose(1, 0, 2).reshape(rank, -1)
     s_bias = small[:, rank].reshape(-1)
     s_group = jnp.sum(small[:, rank + 1 : used], axis=0).reshape(-1)[:DV]
-    cuts = [key_cols, 2 * key_cols, 2 * key_cols + val_cols, attn_cols, attn_cols + val_cols]
-    cuts = cuts + [cuts[-1] + hidden, cuts[-1] + 2 * hidden]
-    s_query, s_key, s_value, s_outgate, s_output, s_gate, s_up, s_down = jnp.split(
-        grads, cuts, axis=1
+    s_query, s_key, s_value, s_outgate = jnp.split(
+        grads_attn, [key_cols, 2 * key_cols, 2 * key_cols + val_cols], axis=1
+    )
+    s_output, s_gate, s_up, s_down = jnp.split(
+        grads_late, [val_cols, val_cols + hidden, val_cols + 2 * hidden], axis=1
     )
     return (
         result.reshape(seqs_here, tok_here, width),

time: 351 us -> 386 us (1.100)
  local copies, waits for them, and re-layouts: 41.5 us -> 74.2 us
  Pallas kernels: 238 us -> 219 us
  other arithmetic: 37.9 us -> 56.6 us
    pallas_call x8 -> x7, Pallas kernels: 238 us -> 219 us  [exchange(): pl.pallas_call(kernel, out_shape=out_shape, in_specs=[vmem] * len(items),...]
    squeeze x8, local copies, waits for them, and re-layouts: 0.11 us -> 7.55 us  [mixer_block(): lax.scan(jax.checkpoint(block_step), start_state, (cut(queries), cut(keys...]
    dynamic_slice x3 -> x0, local copies, waits for them, and re-layouts: 5.84 us -> none  [my_rows(): array = lax.dynamic_index_in_dim(array, dp_pos, 2, False)]
    unnamed x98 -> x92, local copies, waits for them, and re-layouts: 14.2 us -> 19.5 us
    reshape x0 -> x2, other arithmetic: none -> 4.53 us  [by_part(): array.transpose(2, 0, 1, 3).reshape(n_dp, total_rows, n_seq * part_rows)]
    reduce_sum x4 -> x1, other arithmetic: 4.96 us -> 0.61 us  [on_device(): jnp.sum(small_all, axis=0)]
    convert_element_type x2 -> x3, local copies, waits for them, and re-layouts: 0.4 us -> 4.7 us  [the longest x2 3.4 us: grad_of(): return dot_rows(all_rows(left), all_rows(right)).astype(bf16)]
where the time goes in v2:
time: 386 us; the launch traced here: 383 us
  Pallas kernels  219 us (57%)
  local copies, waits for them, and re-layouts  74.2 us (19%)
  other arithmetic  56.6 us (15%)
  matrix products  31.2 us (8%)
    pallas_call x7, Pallas kernels, exchange(): pl.pallas_call(kernel, out_shape=out_shape, in_specs=[vmem] * len(items),...  219 us
    unnamed x92, local copies, waits for them, and re-layouts  19.5 us
    dot_general x6, other arithmetic, block_step(): jnp.einsum('id,jd,ijd->ij', query_blk, key_blk, spread, precision=highest)  11.3 us
    dot_general x5, matrix products, dot_rows(): lax.dot_general(left, right, (((0,), (0,)), ((), ())), preferred_element_...  8.42 us

profile of v2, /device:TPU:0, one launch (start us, length us, event | category | flops | bytes accessed | tf_op | source)
XLA Modules:
  0.0 382.5 jit_solution(1848407320587304026)
XLA Ops:
  5.9 30.6 %shard_map.279 = bf16[4,256,1152]{2,1,0:T(8,128)(2,1)} custom-call(bf16[256,1152]{1,0:T(8,128)(2,1)} %concatenate.39.refs_0_), custom_call_target="tpu_custom_call" | custom-call | tf_op jit(solution)/shard_map/pallas_call | solution.py:355
  36.5 2.4 slice_convert_fusion
  45.7 11.6 %shard_map.280 = (bf16[4,128,256]{2,1,0:T(8,128)(2,1)}, f32[4,8,128]{2,1,0:T(8,128)}) custom-call(bf16[128,256]{1,0:T(8,128)(2,1)} %convolution_convert_fusion.2.refs_0_, f32[8,128]{1,0:T(8,128)} %broadcast_in_dim.117.refs_1_), custom_call_target="tpu_custom_call" | custom-call | tf_op jit(solution)/shard_map/pallas_call | solution.py:355
  61.5 14.2 %while.40 = (s32[]{:T(128)}, f32[1,1,128,256]{3,2,1,0:T(8,128)S(1)}, f32[2,1,1,64,256]{4,3,2,1,0:T(8,128)}, f32[2,1,1,128,256]{4,3,2,1,0:T(8,128)S(1)}, f32[2,1,...) while((s32[]{:T(128)}, ...), condition=%wide.region_4.5_spmd.clone.clone, body=%wide.region_2.4_spmd.clone.sunk.clone | while | flops 66686976 | bytes 6804649 | solution.py:421
  79.5 1.9 copy.209
  81.5 1.9 copy.210
  85.3 3.4 concatenate.40.refs_1_
  88.6 45.4 %shard_map.281 = (bf16[4,32,1024]{2,1,0:T(8,128)(2,1)}, bf16[4,256,2112]{2,1,0:T(8,128)(2,1)}) custom-call(bf16[4,32,1024]{2,1,0:T(8,128)(2,1)} %bitcast.677, bf16[256,2112]{1,0:T(8,128)(2,1)} %concatenate.40.refs_1_), custom_call_target="tpu_custom_call" | custom-call | tf_op jit(solution)/shard_map/pallas_call | solution.py:355
  137.1 2.8 fusion.78
  145.5 2.0 copy.214
  148.9 2.0 copy_bitcast_fusion.1.refs_1_
  150.9 2.1 copy.217
  158.3 19.9 %shard_map.282 = (bf16[4,64,1024]{2,1,0:T(8,128)(2,1)}, bf16[2,128,512]{2,1,0:T(8,128)(2,1)}, bf16[2,128,512]{2,1,0:T(8,128)(2,1)}, bf16[2,128,1408]{2,1,0:T(8,128)(2,1)}, bf16[2,128,704]{2,1,0:T(8,128)(2,1)}) custom-call(bf16[4,64,1024]{2,1,0:T(8,128)(2,1)} %bitcast.672, bf16[2,128,512]{2,1,0:T(8,128)(2,1)} %copy_bitcast_fusion.1.refs_1_, ...), custom_call_target="tpu_custom_call" | custom-call | tf_op jit(solution)/shard_map/pallas_call | solution.py:355
  183.4 2.3 copy.226
  185.7 3.0 fusion.75
  191.9 2.0 copy.220
  193.9 2.3 squeeze.91
  196.2 2.5 copy_bitcast_fusion.refs_2_
  198.7 10.2 %shard_map.283 = (bf16[4,128,256]{2,1,0:T(8,128)(2,1)}, bf16[2,128,256]{2,1,0:T(8,128)(2,1)}, bf16[2,128,512]{2,1,0:T(8,128)(2,1)}) custom-call(bf16[128,256]{1,0:T(8,128)(2,1)} %convolution_convert_fusion.1.refs_0_, bf16[128,256]{1,0:T(8,128)(2,1)} %copy-done.23, bf16[2,128,512]{2,1,0:T(8,128)(2,1)} %copy_bitcast_fusion.refs_2_), custom_call_target="tpu_custom_call" | custom-call | tf_op jit(solution)/shard_map/pallas_call | solution.py:355
  208.9 2.0 fusion.89
  212.0 3.3 pad_maximum_fusion
  218.9 30.2 %while.41 = (s32[]{:T(128)}, f32[1,1,128,256]{2,3,1,0:T(8,128)S(1)}, f32[2,1,1,64,128]{4,3,2,1,0:T(8,128)}, bf16[2,1,1,64,128]{4,3,2,1,0:T(8,128)(2,1)}, bf16[2,...) while((s32[]{:T(128)}, ...), condition=%wide.region_16.17_spmd.clone.clone, body=%wide.region_9.16_spmd.clone.sunk.clone | while | flops 141848576 | bytes 5366129 | solution.py:421
  225.0 2.0 fusion.298
  227.2 2.0 fusion.300
  229.9 2.3 fusion.303
  240.1 2.0 fusion.298
  242.3 2.0 fusion.300
  245.0 2.3 fusion.303
  253.8 1.9 fusion.123
  258.4 68.3 %shard_map.284 = (f32[2,128,2368]{2,1,0:T(8,128)}, bf16[4,32,1152]{2,1,0:T(8,128)(2,1)}, f32[8,24,128]{2,1,0:T(8,128)}, bf16[2,128,512]{2,1,0:T(8,128)(2,1)}, bf16[2,128,768]{2,1,0:T(8,128)(2,1)}) custom-call(bf16[4,128,2368]{2,1,0:T(8,128)(2,1)} %bitcast.660, bf16[4,32,1152]{2,1,0:T(8,128)(2,1)} %concatenate.47.refs_1_, ...), custom_call_target="tpu_custom_call" | custom-call | tf_op jit(solution)/shard_map/pallas_call | solution.py:355
  333.2 32.6 %shard_map.285 = (f32[2,128,768]{2,1,0:T(8,128)}, f32[8,24,256]{2,1,0:T(8,128)}, f32[4,24,128]{2,1,0:T(8,128)}) custom-call(bf16[4,128,768]{2,1,0:T(8,128)(2,1)} %bitcast.668, f32[4,24,256]{2,1,0:T(8,128)} %maximum_bitcast_fusion.refs_1_, f32[24,128]{1,0:T(8,128)} %reduce_sum.179.refs_2_), custom_call_target="tpu_custom_call" | custom-call | tf_op jit(solution)/shard_map/pallas_call | solution.py:355
  377.2 2.0 fusion.169
  (282 shorter events, 110.0 us)
Async XLA Ops:
  0.6 41.1 %copy-start = (f32[16,512]{1,0:T(8,128)S(1)}, f32[16,512]{1,0:T(8,128)}, u32[]{:S(2)}) copy-start(f32[16,512]{1,0:T(8,128)} %param.28) | copy-start | bytes 98308
  5.9 34.2 %copy-start.1 = (f32[1,128,1024]{2,1,0:T(8,128)S(1)}, f32[1,128,1024]{2,1,0:T(8,128)}, u32[]{:S(2)}) copy-start(f32[1,128,1024]{2,1,0:T(8,128)} %param.20) | copy-start | bytes 1572868
  36.5 4.3 %copy-start.2 = (bf16[4,256,1152]{2,1,0:T(8,128)(2,1)S(1)}, bf16[4,256,1152]{2,1,0:T(8,128)(2,1)}, u32[]{:S(2)}) copy-start(bf16[4,256,1152]{2,1,0:T(8,128)(2,1)} %shard_map.279) | copy-start | bytes 7077892
  40.8 17.2 %copy-start.40 = (f32[128]{0:T(128)}, f32[128]{0:T(128)S(1)}, u32[]{:S(2)}) copy-start(f32[128]{0:T(128)S(1)} %get-tuple-element.616) | copy-start | bytes 1540
  42.1 18.5 %copy-start.19 = (f32[128,128]{1,0:T(8,128)}, f32[128,128]{1,0:T(8,128)S(1)}, u32[]{:S(2)}) copy-start(f32[128,128]{1,0:T(8,128)S(1)} %convolution_add_fusion.3) | copy-start | bytes 196612
  42.9 17.6 %copy-start.21 = (f32[1,1,128,128]{3,2,1,0:T(8,128)}, f32[1,1,128,128]{3,2,1,0:T(8,128)S(1)}, u32[]{:S(2)}) copy-start(f32[1,1,128,128]{3,2,1,0:T(8,128)S(1)} %reduce_window_sum.52) | copy-start | bytes 196612
  61.5 15.4 %copy-start.43 = (f32[256]{0:T(256)S(1)}, f32[256]{0:T(256)}, u32[]{:S(2)}) copy-start(f32[256]{0:T(256)} %param.30) | copy-start | bytes 3076
  64.5 3.1 copy-start.15
  71.6 3.1 copy-start.15
  75.6 13.0 %copy-start.13 = (f32[2,1,1,128,256]{4,3,2,1,0:T(8,128)}, f32[2,1,1,128,256]{4,3,2,1,0:T(8,128)S(1)}, u32[]{:S(2)}) copy-start(f32[2,1,1,128,256]{4,3,2,1,0:T(8,128)S(1)} %get-tuple-element.881) | copy-start | bytes 786436
  134.0 7.9 %slice-start = ((s8[4456448]{0:T(1024)(128)(4,1)}), s8[262144]{0:T(1024)(128)(4,1)S(1)}, s32[]{:S(2)}) async-start(s8[4456448]{0:T(1024)(128)(4,1)} %bitcast.714), calls=%async_computation | async-start | bytes 524288
  137.1 4.8 %slice-start.1 = ((s8[4456448]{0:T(1024)(128)(4,1)}), s8[4194304]{0:T(1024)(128)(4,1)S(1)}, s32[]{:S(2)}) async-start(s8[4456448]{0:T(1024)(128)(4,1)} %bitcast.714), calls=%async_computation.1 | async-start | bytes 8388608
  143.7 3.9 %copy-start.8 = (bf16[4,32,1024]{2,1,0:T(8,128)(2,1)S(1)}, bf16[4,32,1024]{2,1,0:T(8,128)(2,1)}, u32[]{:S(2)}) copy-start(bf16[4,32,1024]{2,1,0:T(8,128)(2,1)} %get-tuple-element.353) | copy-start | bytes 786436
  183.4 5.3 %copy-start.6 = (f32[128,768]{1,0:T(8,128)S(1)}, f32[128,768]{1,0:T(8,128)}, u32[]{:S(2)}) copy-start(f32[128,768]{1,0:T(8,128)} %copy-done.5) | copy-start | bytes 1179652
  185.7 5.2 %copy-start.22 = (f32[1,1,128,128]{3,2,1,0:T(8,128)S(1)}, f32[1,1,128,128]{3,2,1,0:T(8,128)}, u32[]{:S(2)}) copy-start(f32[1,1,128,128]{3,2,1,0:T(8,128)} %copy-done.21) | copy-start | bytes 196612
  224.5 4.7 %copy-start.26 = (f32[2,1,1,64,128]{4,3,2,1,0:T(8,128)S(1)}, f32[2,1,1,64,128]{4,3,2,1,0:T(8,128)}, u32[]{:S(2)}) copy-start(f32[2,1,1,64,128]{4,3,2,1,0:T(8,128)} %get-tuple-element.889) | copy-start | bytes 196612 | tf_op jit(solution)/shard_map/transpose(jvp(vmap(vmap())))/while
  224.5 4.7 %copy-start.35 = (bf16[2,1,1,64,128]{4,3,2,1,0:T(8,128)(2,1)S(1)}, bf16[2,1,1,64,128]{4,3,2,1,0:T(8,128)(2,1)}, u32[]{:S(2)}) copy-start(bf16[2,1,1,64,128]{4,3,2,1,0:T(8,128)(2,1)} %get-tuple-element.890) | copy-start | bytes 98308 | tf_op jit(solution)/shard_map/transpose(jvp(vmap(vmap())))/while
  224.5 5.4 %copy-start.18 = (f32[64,64]{1,0:T(8,128)S(1)}, f32[64,64]{1,0:T(8,128)}, u32[]{:S(2)}) copy-start(f32[64,64]{1,0:T(8,128)} %fusion.294) | copy-start | bytes 49156 | tf_op jit(solution)/shard_map/transpose(jvp(vmap(vmap())))/while
  224.8 7.4 %copy-start.29 = (bf16[2,1,1,64,256]{4,3,2,1,0:T(8,128)(2,1)S(1)}, bf16[2,1,1,64,256]{4,3,2,1,0:T(8,128)(2,1)}, u32[]{:S(2)}) copy-start(bf16[2,1,1,64,256]{4,3,2,1,0:T(8,128)(2,1)} %get-tuple-element.891) | copy-start | bytes 196612 | tf_op jit(solution)/shard_map/transpose(jvp(vmap(vmap())))/while
  239.6 4.7 %copy-start.26 = (f32[2,1,1,64,128]{4,3,2,1,0:T(8,128)S(1)}, f32[2,1,1,64,128]{4,3,2,1,0:T(8,128)}, u32[]{:S(2)}) copy-start(f32[2,1,1,64,128]{4,3,2,1,0:T(8,128)} %get-tuple-element.889) | copy-start | bytes 196612 | tf_op jit(solution)/shard_map/transpose(jvp(vmap(vmap())))/while
  239.6 4.7 %copy-start.35 = (bf16[2,1,1,64,128]{4,3,2,1,0:T(8,128)(2,1)S(1)}, bf16[2,1,1,64,128]{4,3,2,1,0:T(8,128)(2,1)}, u32[]{:S(2)}) copy-start(bf16[2,1,1,64,128]{4,3,2,1,0:T(8,128)(2,1)} %get-tuple-element.890) | copy-start | bytes 98308 | tf_op jit(solution)/shard_map/transpose(jvp(vmap(vmap())))/while
  239.6 5.4 %copy-start.18 = (f32[64,64]{1,0:T(8,128)S(1)}, f32[64,64]{1,0:T(8,128)}, u32[]{:S(2)}) copy-start(f32[64,64]{1,0:T(8,128)} %fusion.294) | copy-start | bytes 49156 | tf_op jit(solution)/shard_map/transpose(jvp(vmap(vmap())))/while
  239.9 7.4 %copy-start.29 = (bf16[2,1,1,64,256]{4,3,2,1,0:T(8,128)(2,1)S(1)}, bf16[2,1,1,64,256]{4,3,2,1,0:T(8,128)(2,1)}, u32[]{:S(2)}) copy-start(bf16[2,1,1,64,256]{4,3,2,1,0:T(8,128)(2,1)} %get-tuple-element.891) | copy-start | bytes 196612 | tf_op jit(solution)/shard_map/transpose(jvp(vmap(vmap())))/while
  249.1 4.0 %copy-start.44 = (f32[256]{0:T(256)S(1)}, f32[256]{0:T(256)}, u32[]{:S(2)}) copy-start(f32[256]{0:T(256)} %get-tuple-element.535) | copy-start | bytes 3076
  249.2 4.6 %copy-start.41 = (f32[128]{0:T(128)S(1)}, f32[128]{0:T(128)}, u32[]{:S(2)}) copy-start(f32[128]{0:T(128)} %copy-done.40) | copy-start | bytes 1540
  251.6 6.1 %copy-start.31 = (bf16[2,1,1,64,256]{4,3,2,1,0:T(8,128)(2,1)S(1)}, bf16[2,1,1,64,256]{4,3,2,1,0:T(8,128)(2,1)}, u32[]{:S(2)}) copy-start(bf16[2,1,1,64,256]{4,3,2,1,0:T(8,128)(2,1)} %get-tuple-element.366) | copy-start | bytes 196612
  251.6 6.1 %copy-start.37 = (bf16[2,1,1,64,128]{4,3,2,1,0:T(8,128)(2,1)S(1)}, bf16[2,1,1,64,128]{4,3,2,1,0:T(8,128)(2,1)}, u32[]{:S(2)}) copy-start(bf16[2,1,1,64,128]{4,3,2,1,0:T(8,128)(2,1)} %get-tuple-element.365) | copy-start | bytes 98308
  251.6 6.1 %copy-start.39 = (bf16[128,256]{1,0:T(8,128)(2,1)S(1)}, bf16[128,256]{1,0:T(8,128)(2,1)}, u32[]{:S(2)}) copy-start(bf16[128,256]{1,0:T(8,128)(2,1)} %get-tuple-element.602) | copy-start | bytes 196612
  258.4 69.8 %copy-start.12 = (f32[128,1024]{1,0:T(8,128)S(1)}, f32[128,1024]{1,0:T(8,128)}, u32[]{:S(2)}) copy-start(f32[128,1024]{1,0:T(8,128)} %bitcast_add_fusion.6) | copy-start | bytes 1572868
  258.4 69.8 %copy-start.45 = (f32[128]{0:T(128)S(1)}, f32[128]{0:T(128)}, u32[]{:S(2)}) copy-start(f32[128]{0:T(128)} %get-tuple-element.615) | copy-start | bytes 1540
  328.2 3.6 copy-start.42
  329.2 3.4 copy-start.38
  (25 other events, 47.8 us)

commit v3 on v2

--- a/solution.py
+++ b/solution.py
@@ -213,12 +213,18 @@
 
                     @pl.when(first)
                     def _():
+                        if step > 0:
+                            before = goal + 1 if way == 0 else goal - 1
+                            hop(way, step - 1, src.at[before], before).wait_send()
                         hop(way, step, src.at[goal], goal).start()
 
-                    guarded(
-                        first,
-                        lambda way=way, goal=goal: hop(way, step, src.at[goal], goal).wait_send(),
-                    )
+                    if step == n - 2:
+                        guarded(
+                            first,
+                            lambda way=way, goal=goal: hop(
+                                way, step, src.at[goal], goal
+                            ).wait_send(),
+                        )
 
                     @pl.when(inner)
                     def _():
@@ -351,6 +357,19 @@
         for wait in waits:
             wait()
 
+    def room(shape, dtype):
+        item = jnp.dtype(dtype).itemsize
+        lead = 1
+        for extent in shape[:-2]:
+            lead *= extent
+        tile = 32 // item
+        return lead * (-(-shape[-2] // tile) * tile) * (-(-shape[-1] // 128) * 128) * item
+
+    total = sum(room(item[2].shape, item[2].dtype) for item in items)
+    total += sum(room(shape.shape, shape.dtype) for shape in out_shape)
+    for kind, _, arr in items:
+        total += room(arr.shape, arr.dtype) * {"ar": 3, "rs": 4}.get(kind, 0)
+    limit = min(60 * 2**20, total + total // 8 + 2 * 2**20)
     vmem = pl.BlockSpec(memory_space=pltpu.VMEM)
     return pl.pallas_call(
         kernel,
@@ -359,7 +378,7 @@
         out_specs=[vmem] * len(items),
         scratch_shapes=scratch,
         compiler_params=pltpu.CompilerParams(
-            collective_id=cid, has_side_effects=True, vmem_limit_bytes=60 * 1024 * 1024
+            collective_id=cid, has_side_effects=True, vmem_limit_bytes=limit
         ),
     )(*[item[2] for item in items])
 

time: 386 us -> 340 us (0.88)
  Pallas kernels: 219 us -> 202 us
  other arithmetic: 56.6 us -> 40.9 us
  matrix products: 31.2 us -> 24.3 us
  local copies, waits for them, and re-layouts: 74.2 us -> 68.9 us
    pallas_call x7, Pallas kernels: 219 us -> 202 us  [exchange(): pl.pallas_call(kernel, out_shape=out_shape, in_specs=[vmem] * len(items),...]
    unnamed x92 -> x152, local copies, waits for them, and re-layouts: 19.5 us -> 34 us
    squeeze x8, local copies, waits for them, and re-layouts: 7.55 us -> 0.11 us  [mixer_block(): lax.scan(jax.checkpoint(block_step), start_state, (cut(queries), cut(keys...]
where the time goes in v3:
time: 340 us; the launch traced here: 339 us
  Pallas kernels  202 us (59%)
  local copies, waits for them, and re-layouts  68.9 us (20%)
  other arithmetic  40.9 us (12%)
  matrix products  24.3 us (7%)
    pallas_call x7, Pallas kernels, exchange(): pl.pallas_call(kernel, out_shape=out_shape, in_specs=[vmem] * len(items),...  202 us
    unnamed x152, local copies, waits for them, and re-layouts  34 us
    dot_general x6, other arithmetic, block_step(): jnp.einsum('id,jd,ijd->ij', query_blk, key_blk, spread, precision=highest)  8.45 us
    dot_general x5, matrix products, dot_t(): lax.dot_general(left, right, (((1,), (1,)), ((), ())), preferred_element_...  6.81 us

profile of v3, /device:TPU:0, one launch (start us, length us, event | category | flops | bytes accessed | tf_op | source)
XLA Modules:
  0.0 338.7 jit_solution(15920169999136778679)
XLA Ops:
  5.2 28.1 %shard_map.279 = bf16[4,256,1152]{2,1,0:T(8,128)(2,1)S(1)} custom-call(bf16[256,1152]{1,0:T(8,128)(2,1)S(1)} %concatenate.39.refs_0_), custom_call_target="tpu_custom_call" | custom-call | tf_op jit(solution)/shard_map/pallas_call | solution.py:374
  38.3 10.0 %shard_map.280 = (bf16[4,128,256]{2,1,0:T(8,128)(2,1)S(1)}, f32[4,8,128]{2,1,0:T(8,128)S(1)}) custom-call(bf16[128,256]{1,0:T(8,128)(2,1)S(1)} %convolution_convert_fusion.2.refs_0_, f32[8,128]{1,0:T(8,128)S(1)} %broadcast_in_dim.117.refs_1_), custom_call_target="tpu_custom_call" | custom-call | tf_op jit(solution)/shard_map/pallas_call | solution.py:374
  50.9 6.8 %while.40 = (s32[]{:T(128)}, f32[1,1,128,256]{3,2,1,0:T(8,128)S(1)}, f32[2,1,1,64,256]{4,3,2,1,0:T(8,128)S(1)}, f32[2,1,1,128,256]{4,3,2,1,0:T(8,128)S(1)}, f32[...) while((s32[]{:T(128)}, ...), condition=%wide.region_4.5_spmd.clone.clone, body=%wide.region_2.4_spmd.clone.sunk.clone | while | flops 66686976 | bytes 5756017 | solution.py:440
  60.6 1.9 copy.209
  62.5 1.9 copy.210
  64.4 1.9 copy.208
  66.3 2.6 concatenate.40.refs_1_
  69.8 42.0 %shard_map.281 = (bf16[4,32,1024]{2,1,0:T(8,128)(2,1)S(1)}, bf16[4,256,2112]{2,1,0:T(8,128)(2,1)S(1)}) custom-call(bf16[4,32,1024]{2,1,0:T(8,128)(2,1)S(1)} %bitcast.657, bf16[256,2112]{1,0:T(8,128)(2,1)S(1)} %concatenate.40.refs_1_), custom_call_target="tpu_custom_call" | custom-call | tf_op jit(solution)/shard_map/pallas_call | solution.py:374
  111.8 2.1 copy-done.20
  117.8 2.5 fusion.78
  120.3 2.0 multiply_convert_fusion.4
  124.8 2.1 copy.213
  126.9 2.0 copy.214
  130.2 2.0 copy_bitcast_fusion.1.refs_1_
  132.2 2.0 copy.217
  136.1 1.8 copy.218
  142.5 17.2 %shard_map.282 = (bf16[4,64,1024]{2,1,0:T(8,128)(2,1)S(1)}, bf16[2,128,512]{2,1,0:T(8,128)(2,1)S(1)}, bf16[2,128,512]{2,1,0:T(8,128)(2,1)S(1)}, bf16[2,128,1408]...) custom-call(bf16[4,64,1024]{2,1,0:T(8,128)(2,1)S(1)} %bitcast.656, bf16[2,128,512]{2,1,0:T(8,128)(2,1)S(1)} %copy-done.6, ...), custom_call_target="tpu_custom_call" | custom-call | tf_op jit(solution)/shard_map/pallas_call | solution.py:374
  165.4 2.4 copy.226
  171.4 2.1 copy.220
  176.5 8.4 %shard_map.283 = (bf16[4,128,256]{2,1,0:T(8,128)(2,1)S(1)}, bf16[2,128,256]{2,1,0:T(8,128)(2,1)S(1)}, bf16[2,128,512]{2,1,0:T(8,128)(2,1)S(1)}) custom-call(bf16[128,256]{1,0:T(8,128)(2,1)S(1)} %convolution_convert_fusion.1.refs_0_, bf16[128,256]{1,0:T(8,128)(2,1)S(1)} %copy-done.13, bf16[2,128,512]{2,1,0:T(8,128)(2,1)S(1)} %copy_bitcast_fusion.refs_2_), custom_call_target="tpu_custom_call" | custom-call | tf_op jit(solution)/shard_map/pallas_call | solution.py:374
  186.1 3.3 pad_maximum_fusion
  191.0 17.5 %while.41 = (s32[]{:T(128)}, f32[1,1,128,256]{2,3,1,0:T(8,128)S(1)}, f32[2,1,1,64,128]{4,3,2,1,0:T(8,128)S(1)}, bf16[2,1,1,64,128]{4,3,2,1,0:T(8,128)(2,1)}, bf1...) while((s32[]{:T(128)}, ...), condition=%wide.region_16.17_spmd.clone.clone, body=%wide.region_9.16_spmd.clone.sunk.clone | while | flops 141848576 | bytes 4776221 | solution.py:440
  196.1 2.3 fusion.303
  204.9 2.3 fusion.303
  209.1 2.3 fusion.90
  217.6 65.9 %shard_map.284 = (f32[2,128,2368]{2,1,0:T(8,128)S(1)}, bf16[4,32,1152]{2,1,0:T(8,128)(2,1)S(1)}, f32[8,24,128]{2,1,0:T(8,128)S(1)}, bf16[2,128,512]{2,1,0:T(8,128)(2,1)S(1)}, bf16[2,128,768]{2,1,0:T(8,128)(2,1)S(1)}) custom-call(bf16[4,128,2368]{2,1,0:T(8,128)(2,1)S(1)} %bitcast.652, bf16[4,32,1152]{2,1,0:T(8,128)(2,1)S(1)} %concatenate.47.refs_1_, ...), custom_call_target="tpu_custom_call" | custom-call | tf_op jit(solution)/shard_map/pallas_call | solution.py:374
  283.5 1.8 fusion.113
  287.6 1.9 copy.274
  290.9 30.9 %shard_map.285 = (f32[2,128,768]{2,1,0:T(8,128)S(1)}, f32[8,24,256]{2,1,0:T(8,128)S(1)}, f32[4,24,128]{2,1,0:T(8,128)S(1)}) custom-call(bf16[4,128,768]{2,1,0:T(8,128)(2,1)S(1)} %bitcast.653, f32[4,24,256]{2,1,0:T(8,128)S(1)} %maximum_bitcast_fusion.refs_1_, f32[24,128]{1,0:T(8,128)S(1)} %reduce_sum.179.refs_2_), custom_call_target="tpu_custom_call" | custom-call | tf_op jit(solution)/shard_map/pallas_call | solution.py:374
  326.6 1.9 fusion.170
  333.1 2.2 copy.281
  335.4 2.2 copy.282
  (321 shorter events, 84.5 us)
Async XLA Ops:
  0.6 35.6 %copy-start = (f32[16,512]{1,0:T(8,128)S(1)}, f32[16,512]{1,0:T(8,128)}, u32[]{:S(2)}) copy-start(f32[16,512]{1,0:T(8,128)} %param.28) | copy-start | bytes 98308
  5.2 29.3 %copy-start.22 = (f32[1,128,1024]{2,1,0:T(8,128)S(1)}, f32[1,128,1024]{2,1,0:T(8,128)}, u32[]{:S(2)}) copy-start(f32[1,128,1024]{2,1,0:T(8,128)} %param.20) | copy-start | bytes 1572868
  35.2 13.8 %copy-start.61 = (f32[128]{0:T(128)}, f32[128]{0:T(128)S(1)}, u32[]{:S(2)}) copy-start(f32[128]{0:T(128)S(1)} %get-tuple-element.616) | copy-start | bytes 1540
  35.4 15.4 %copy-start.59 = (f32[128,16]{0,1:T(8,128)}, f32[128,16]{0,1:T(8,128)S(1)}, u32[]{:S(2)}) copy-start(f32[128,16]{0,1:T(8,128)S(1)} %fusion.129) | copy-start | bytes 24580
  37.1 11.9 %copy-start.49 = (f32[1,1,128,128]{3,2,1,0:T(8,128)}, f32[1,1,128,128]{3,2,1,0:T(8,128)S(1)}, u32[]{:S(2)}) copy-start(f32[1,1,128,128]{3,2,1,0:T(8,128)S(1)} %reduce_window_sum.52) | copy-start | bytes 196612
  50.8 7.1 %copy-start.68 = (f32[256]{0:T(256)S(1)}, f32[256]{0:T(256)}, u32[]{:S(2)}) copy-start(f32[256]{0:T(256)} %param.30) | copy-start | bytes 3076
  57.7 8.6 %copy-start.25 = (f32[2,1,1,64,256]{4,3,2,1,0:T(8,128)}, f32[2,1,1,64,256]{4,3,2,1,0:T(8,128)S(1)}, u32[]{:S(2)}) copy-start(f32[2,1,1,64,256]{4,3,2,1,0:T(8,128)S(1)} %get-tuple-element.911) | copy-start | bytes 393220
  57.7 8.6 %copy-start.29 = (f32[2,1,1,64,128]{4,3,2,1,0:T(8,128)}, f32[2,1,1,64,128]{4,3,2,1,0:T(8,128)S(1)}, u32[]{:S(2)}) copy-start(f32[2,1,1,64,128]{4,3,2,1,0:T(8,128)S(1)} %get-tuple-element.912) | copy-start | bytes 196612
  57.7 8.6 %copy-start.31 = (f32[2,1,1,64,128]{4,3,2,1,0:T(8,128)}, f32[2,1,1,64,128]{4,3,2,1,0:T(8,128)S(1)}, u32[]{:S(2)}) copy-start(f32[2,1,1,64,128]{4,3,2,1,0:T(8,128)S(1)} %get-tuple-element.913) | copy-start | bytes 196612
  57.7 8.6 %copy-start.38 = (f32[2,1,1,64,128]{4,3,2,1,0:T(8,128)}, f32[2,1,1,64,128]{4,3,2,1,0:T(8,128)S(1)}, u32[]{:S(2)}) copy-start(f32[2,1,1,64,128]{4,3,2,1,0:T(8,128)S(1)} %get-tuple-element.914) | copy-start | bytes 196612
  57.7 8.6 %copy-start.44 = (f32[2,1,1,128,256]{4,3,2,1,0:T(8,128)}, f32[2,1,1,128,256]{4,3,2,1,0:T(8,128)S(1)}, u32[]{:S(2)}) copy-start(f32[2,1,1,128,256]{4,3,2,1,0:T(8,128)S(1)} %get-tuple-element.881) | copy-start | bytes 786436
  57.7 8.6 %copy-start.45 = (f32[2,1,1,64,256]{4,3,2,1,0:T(8,128)}, f32[2,1,1,64,256]{4,3,2,1,0:T(8,128)S(1)}, u32[]{:S(2)}) copy-start(f32[2,1,1,64,256]{4,3,2,1,0:T(8,128)S(1)} %get-tuple-element.352) | copy-start | bytes 393220
  124.8 4.2 %copy-start.5 = (bf16[4,32,1024]{2,1,0:T(8,128)(2,1)S(1)}, bf16[4,32,1024]{2,1,0:T(8,128)(2,1)}, u32[]{:S(2)}) copy-start(bf16[4,32,1024]{2,1,0:T(8,128)(2,1)} %copy-done.4) | copy-start | bytes 786436
  142.5 19.0 %copy-start.23 = (f32[1,128,1024]{2,1,0:T(8,128)S(1)}, f32[1,128,1024]{2,1,0:T(8,128)}, u32[]{:S(2)}) copy-start(f32[1,128,1024]{2,1,0:T(8,128)} %param.20) | copy-start | bytes 1572868
  163.1 4.6 %copy-start.11 = (bf16[2,128,1408]{2,1,0:T(8,128)(2,1)S(1)}, bf16[2,128,1408]{2,1,0:T(8,128)(2,1)}, u32[]{:S(2)}) copy-start(bf16[2,128,1408]{2,1,0:T(8,128)(2,1)} %copy-done.10) | copy-start | bytes 2162692
  163.1 4.6 %copy-start.15 = (bf16[2,128,512]{2,1,0:T(8,128)(2,1)S(1)}, bf16[2,128,512]{2,1,0:T(8,128)(2,1)}, u32[]{:S(2)}) copy-start(bf16[2,128,512]{2,1,0:T(8,128)(2,1)} %copy-done.14) | copy-start | bytes 786436
  171.4 5.1 %copy-start.13 = (bf16[128,256]{1,0:T(8,128)(2,1)S(1)}, bf16[128,256]{1,0:T(8,128)(2,1)}, u32[]{:S(2)}) copy-start(bf16[128,256]{1,0:T(8,128)(2,1)} %copy-done.12) | copy-start | bytes 196612
  186.0 4.9 %copy-start.26 = (f32[2,1,1,64,256]{4,3,2,1,0:T(8,128)S(1)}, f32[2,1,1,64,256]{4,3,2,1,0:T(8,128)}, u32[]{:S(2)}) copy-start(f32[2,1,1,64,256]{4,3,2,1,0:T(8,128)} %copy-done.25) | copy-start | bytes 393220
  186.0 4.9 %copy-start.30 = (f32[2,1,1,64,128]{4,3,2,1,0:T(8,128)S(1)}, f32[2,1,1,64,128]{4,3,2,1,0:T(8,128)}, u32[]{:S(2)}) copy-start(f32[2,1,1,64,128]{4,3,2,1,0:T(8,128)} %copy-done.29) | copy-start | bytes 196612
  186.1 4.9 %copy-start.32 = (f32[2,1,1,64,128]{4,3,2,1,0:T(8,128)S(1)}, f32[2,1,1,64,128]{4,3,2,1,0:T(8,128)}, u32[]{:S(2)}) copy-start(f32[2,1,1,64,128]{4,3,2,1,0:T(8,128)} %copy-done.31) | copy-start | bytes 196612
  186.1 4.9 %copy-start.39 = (f32[2,1,1,64,128]{4,3,2,1,0:T(8,128)S(1)}, f32[2,1,1,64,128]{4,3,2,1,0:T(8,128)}, u32[]{:S(2)}) copy-start(f32[2,1,1,64,128]{4,3,2,1,0:T(8,128)} %copy-done.38) | copy-start | bytes 196612
  192.5 5.9 %copy-start.53 = (bf16[2,1,1,64,256]{4,3,2,1,0:T(8,128)(2,1)S(1)}, bf16[2,1,1,64,256]{4,3,2,1,0:T(8,128)(2,1)}, u32[]{:S(2)}) copy-start(bf16[2,1,1,64,256]{4,3,2,1,0:T(8,128)(2,1)} %get-tuple-element.891) | copy-start | bytes 196612 | tf_op jit(solution)/shard_map/transpose(jvp(vmap(vmap())))/while
  201.2 5.9 %copy-start.53 = (bf16[2,1,1,64,256]{4,3,2,1,0:T(8,128)(2,1)S(1)}, bf16[2,1,1,64,256]{4,3,2,1,0:T(8,128)(2,1)}, u32[]{:S(2)}) copy-start(bf16[2,1,1,64,256]{4,3,2,1,0:T(8,128)(2,1)} %get-tuple-element.891) | copy-start | bytes 196612 | tf_op jit(solution)/shard_map/transpose(jvp(vmap(vmap())))/while
  208.4 4.4 %copy-start.60 = (f32[128,16]{0,1:T(8,128)S(1)}, f32[128,16]{0,1:T(8,128)}, u32[]{:S(2)}) copy-start(f32[128,16]{0,1:T(8,128)} %copy-done.59) | copy-start | bytes 24580
  209.1 4.8 %copy-start.35 = (f32[1,128,1024]{1,2,0:T(8,128)S(1)}, f32[1,128,1024]{1,2,0:T(8,128)}, u32[]{:S(2)}) copy-start(f32[1,128,1024]{1,2,0:T(8,128)} %copy.213) | copy-start | bytes 1572868
  209.1 4.8 %copy-start.56 = (bf16[2,1,1,64,128]{4,3,2,1,0:T(8,128)(2,1)}, bf16[2,1,1,64,128]{4,3,2,1,0:T(8,128)(2,1)S(1)}, u32[]{:S(2)}) copy-start(bf16[2,1,1,64,128]{4,3,2,1,0:T(8,128)(2,1)S(1)} %multiply_convert_fusion.9) | copy-start | bytes 98308
  214.9 68.6 %copy-start.62 = (f32[128]{0:T(128)S(1)}, f32[128]{0:T(128)}, u32[]{:S(2)}) copy-start(f32[128]{0:T(128)} %copy-done.61) | copy-start | bytes 1540
  217.6 67.8 %copy-start.24 = (f32[1,128,1024]{2,1,0:T(8,128)S(1)}, f32[1,128,1024]{2,1,0:T(8,128)}, u32[]{:S(2)}) copy-start(f32[1,128,1024]{2,1,0:T(8,128)} %param.20) | copy-start | bytes 1572868
  217.6 67.8 %copy-start.43 = (f32[128,1024]{1,0:T(8,128)S(1)}, f32[128,1024]{1,0:T(8,128)}, u32[]{:S(2)}) copy-start(f32[128,1024]{1,0:T(8,128)} %bitcast_add_fusion.6) | copy-start | bytes 1572868
  217.6 67.8 %copy-start.72 = (f32[128]{0:T(128)S(1)}, f32[128]{0:T(128)}, u32[]{:S(2)}) copy-start(f32[128]{0:T(128)} %get-tuple-element.615) | copy-start | bytes 1540
  285.4 5.4 %copy-start.63 = (f32[1024]{0:T(1024)S(1)}, f32[1024]{0:T(1024)}, u32[]{:S(2)}) copy-start(f32[1024]{0:T(1024)} %get-tuple-element.533) | copy-start | bytes 12292
  287.6 43.2 %copy-start.3 = (f32[2,128,2368]{2,1,0:T(8,128)S(1)}, f32[2,128,2368]{2,1,0:T(8,128)}, u32[]{:S(2)}) copy-start(f32[2,128,2368]{2,1,0:T(8,128)} %copy-done.2) | copy-start | bytes 7274500
  (45 other events, 92.7 us)
